TPU v7x, 128 devices: a whole 4x4x4 slice. The times are simulated.
128 devices in a mesh: gx: 8 (over y, core), gy: 16 (over z, x).
Axes of the slice: x: 4, y: 4, z: 4, core: 2. Of those that a mesh axis runs over, the one named last changes fastest.
Arguments:
- z_factor: float32 [8, 16, 24, 128, 128], P('gx', 'gy'), may hold values from -1 to 1
- fock: float32 [8, 16, 24, 128, 128], P('gx', 'gy'), may hold values from -1 to 1
- cotangent: float32 [8, 16, 24, 128, 128], P('gx', 'gy'), may hold values from -1 to 1
- tasks_zg: int32 [8, 16, 3, 64], P('gx', 'gy'), may hold values from 0 to 119, as said below
- tasks_fock: int32 [8, 16, 3, 64], P('gx', 'gy'), may hold values from 0 to 119, as said below
- tasks_fz: int32 [8, 16, 3, 64], P('gx', 'gy'), may hold values from 0 to 119, as said below
- tasks_zgt: int32 [8, 16, 3, 64], P('gx', 'gy'), may hold values from 0 to 119, as said below
- tasks_trans: int32 [8, 16, 3, 64], P('gx', 'gy'), may hold values from 0 to 119, as said below
Outputs:
- fock_grad: float32 [8, 16, 24, 128, 128], P('gx', 'gy')
- factor_grad: float32 [8, 16, 24, 128, 128], P('gx', 'gy')
Inputs may be any that keep to these rules, and one draw needn't show every extreme that they name: `tasks_zg`: each cell column's list holds live entries (out below 24) first and then padding entries (out = 24, a = b = 0); out below 24 and a below 24 on live entries, b below 120; the busiest cell column's list is full. `tasks_fock`: each cell column's list holds live entries (out below 24) first and then padding entries (out = 24, a = b = 0); out below 24 and a below 24 on live entries, b below 120; the busiest cell column's list is full. `tasks_fz`: each cell column's list holds live entries (out below 24) first and then padding entries (out = 24, a = b = 0); out below 24 and a below 24 on live entries, b below 120; the busiest cell column's list is full. `tasks_zgt`: each cell column's list holds live entries (out below 24) first and then padding entries (out = 24, a = b = 0); out below 24 and a below 24 on live entries, b below 120; the busiest cell column's list is full. `tasks_trans`: each cell column's list holds live entries (out below 24) first and then padding entries (out = 24, a = b = 0); a and b below 120 and a // 24 = b // 24 on every entry; the busiest cell column's list is full.
All inputs are finite; a program needn't handle non-finite values.
Results may differ from a plain program's by a relative error of at most 0.0003.
Values sent between devices are 32-bit elements; how exact they have to be, the bound alone decides.
A program may use at most 192 MiB of HBM per device.

v0:
```python
import functools

import jax
import jax.numpy as jnp
from jax import lax
from jax.experimental import pallas as pl
from jax.experimental.pallas import tpu as pltpu
from jax.sharding import PartitionSpec as P


TILE = 128
UNROLL = 8
F32 = jnp.float32
I32 = jnp.int32
MESH = pl.DeviceIdType.MESH
STEPS = (("gx", -1), ("gx", 1), ("gy", -1), ("gy", 1))


def split(tile):
    high = tile.astype(jnp.bfloat16)
    low = (tile - high.astype(F32)).astype(jnp.bfloat16)
    return jnp.concatenate([high, low], axis=1)


def product(left, right, turned):
    if turned:
        high, low = right[:, :TILE], right[:, TILE:]
        rows = jnp.concatenate([high, low], axis=0)
        operand = jnp.concatenate([rows, rows], axis=1)
        both = lax.dot_general(left, operand, (((1,), (1,)), ((), ())), preferred_element_type=F32)
    else:
        operand = jnp.concatenate([right, right], axis=0)
        both = lax.dot_general(left, operand, (((1,), (0,)), ((), ())), preferred_element_type=F32)
    return both[:, :TILE] + both[:, TILE:]


def run_list(count, entry, left_of, right_of, turned, total, unroll=UNROLL):
    def step(turn, _):
        entries = [entry(turn * unroll + i) for i in range(unroll)]
        values = [product(left_of(a), right_of(b), turned) for _, a, b in entries]
        for (t, _, _), value in zip(entries, values):
            total[t] += value
        return 0

    lax.fori_loop(0, (count + unroll - 1) // unroll, step, 0)


def live_count(tasks, per_cell):
    length = tasks.shape[2]
    return lax.while_loop(
        lambda n: jnp.logical_and(n < length, tasks[0, 0, jnp.minimum(n, length - 1)] < per_cell),
        lambda n: n + 1,
        jnp.int32(0),
    )


def split_all(source, target, per_cell):
    def step(i, _):
        target[i] = split(source[i])
        return 0

    lax.fori_loop(0, per_cell, step, 0)


def moved_entry(tasks, plan, at):
    return lambda e: (tasks[0, 0, e], tasks[1, 0, e], plan[at, e])


def fetch(sources, grown, sems):
    copies = [
        pltpu.make_async_copy(src, grown.at[pl.ds(at, src.shape[0])], sems.at[i]) for i, (src, at) in enumerate(sources)
    ]
    for c in copies:
        c.start()
    return copies


FOCK_ROW, FZ_ROW, MAP_ROW, ZG_ROW, ZGT_ROW, LIST_ROW, PLAN_ROWS = 0, 1, 2, 6, 7, 8, 32


class Tables:
    def __init__(self, per_cell, length):
        self.per_cell, self.length = per_cell, length
        self.row = lax.broadcasted_iota(I32, (per_cell, length), 0)
        self.lane = lax.broadcasted_iota(I32, (1, TILE), 1)
        self.number = lax.broadcasted_iota(I32, (per_cell, TILE), 0)

    def hits(self, key):
        return jnp.broadcast_to(key, self.row.shape) == self.row

    def named(self, keys, first=0):
        found = sum(self.hits(key).astype(I32) for key in keys)
        found = jnp.where(self.row >= first, found, 0)
        return jnp.minimum(jnp.max(found, axis=1, keepdims=True), 1)

    def of_cell(self, lists, k, first=0):
        return self.named([tasks[2] - k * self.per_cell for tasks in lists], first)

    def inside(self, tasks, k):
        a = tasks[1]
        here = jnp.logical_and(a >= k * self.per_cell, a < (k + 1) * self.per_cell)
        return jnp.logical_and(here, tasks[0] < self.per_cell)

    def outs(self, tasks, k):
        return jnp.where(self.inside(tasks, k), tasks[0], self.per_cell)

    def ranked(self, found):
        square = (self.per_cell, self.per_cell)
        below = (lax.broadcasted_iota(I32, square, 1) < lax.broadcasted_iota(I32, square, 0)).astype(F32)
        return jnp.dot(below, jnp.broadcast_to(found, self.number.shape).astype(F32), preferred_element_type=F32)

    def packed_rows(self, found):
        spread = jnp.broadcast_to(self.lane, self.number.shape).astype(F32)
        here = jnp.logical_and(self.ranked(found) == spread, jnp.broadcast_to(found, self.number.shape) == 1)
        order = jnp.sum(jnp.where(here, self.number, 0), axis=0, keepdims=True)
        return jnp.where(self.lane == TILE - 1, jnp.sum(found), order)

    def rank_of(self, key, found):
        rank = self.ranked(found)[:, : self.length].astype(I32)
        return jnp.sum(jnp.where(self.hits(key), rank, 0), axis=0, keepdims=True)

    def places(self, tasks, lists, first=0):
        place = tasks[2]
        for k in (3, 4):
            key = tasks[2] - k * self.per_cell
            here = jnp.logical_and(key >= first, key < self.per_cell)
            rank = self.rank_of(key, self.of_cell(lists, k, first))
            place = jnp.where(here, k * self.per_cell + first + rank, place)
        return place


def by_quarter(lane, values):
    result = values[3]
    for i in (2, 1, 0):
        result = jnp.where(lane < (i + 1) * (TILE // 4), values[i], result)
    return result


def meet_kernel(tzg, tfock, tfz, tzgt, ttrans, g, *refs, rooms, g_rooms, lead, cuts):
    packs = 2 * len(g_rooms)
    ga, tn, fn, zl, gp = refs[:2], refs[2:6], refs[6:8], refs[8:10], refs[10 : 10 + packs]
    (level, gl, gt, msg, line, lines, pick, picked, gv, packed, bulk_s, bulk_r, list_s, list_r) = refs[10 + packs : 24 + packs]
    line_s, line_r, lines_s, lines_r, own, put = refs[24 + packs :]
    ny, nx = line.shape[0], lines.shape[0]
    per_cell = g.shape[0]
    ix, iy = lax.axis_index("gx"), lax.axis_index("gy")
    barrier = pltpu.get_barrier_semaphore()
    for j in range(1, nx):
        pl.semaphore_signal(barrier, inc=1, device_id=(lax.rem(ix + j, nx), iy), device_id_type=MESH)
    for j in range(1, ny):
        pl.semaphore_signal(barrier, inc=1, device_id=(ix, lax.rem(iy + j, ny)), device_id_type=MESH)
    load = pltpu.make_async_copy(g.at[pl.ds(lead, per_cell - lead)], gv, own.at[3])
    load.start()
    others = []
    for axis, by in STEPS:
        others.append((lax.rem(ix + by + nx, nx), iy) if axis == "gx" else (ix, lax.rem(iy + by + ny, ny)))
    pl.semaphore_wait(barrier, nx + ny - 2)

    lists = []
    for i in range(2):
        lists += [(tzg, gl.at[i], others[2 + i]), (tzgt, gt.at[i], others[2 + i])]
        lists += [(tfock, fn[i], others[2 + i]), (tfz, zl[i], others[2 + i])]
    lists += [(ttrans, tn[k], others[k]) for k in range(4)]
    small = []
    for i, (src, dst, to) in enumerate(lists):
        small.append(pltpu.make_async_remote_copy(src, dst, list_s.at[i], list_r.at[i], device_id=to, device_id_type=MESH))
        small[-1].start()

    def bulk(i, k, start, size):
        part = pl.ds(start, size)
        return pltpu.make_async_remote_copy(
            g.at[part], ga[(k ^ 1) - 2].at[part], bulk_s.at[i], bulk_r.at[i], device_id=others[k], device_id_type=MESH
        )

    large = [bulk(0, 2, 0, cuts), bulk(1, 3, 0, cuts)]
    for c in large:
        c.start()

    tables = Tables(per_cell, tfock.shape[2])

    def most(found):
        return functools.reduce(jnp.maximum, [jnp.sum(v) for v in found])

    needs = (
        most([tables.of_cell((tzg, tzgt), k, lead) for k in (3, 4)]),
        most([tables.of_cell((tfock, tfz), k) for k in (3, 4)]),
        most([tables.named((tables.outs(ttrans, k),)) for k in (1, 2)]),
        most([tables.named((tables.outs(ttrans, k),)) for k in (3, 4)]),
    )
    msg[...] = by_quarter(tables.lane, needs)
    keep = pltpu.make_async_copy(msg, line.at[pl.ds(0, 1)], own.at[0])
    keep.start()
    keep.wait()
    first = []
    for j in range(1, ny):
        to = (ix, lax.rem(iy + j, ny))
        row = line.at[pl.ds(0, 1)]
        first.append(pltpu.make_async_remote_copy(row, line.at[pl.ds(j, 1)], line_s.at[j], line_r.at[j], device_id=to, device_id_type=MESH))
        first[-1].start()
    rest = [bulk(2, 2, cuts, lead - cuts), bulk(3, 3, cuts, lead - cuts)]
    for c in rest:
        c.start()
    for c in first:
        c.wait()
    keep = pltpu.make_async_copy(line, lines.at[0], own.at[1])
    keep.start()
    second = []
    for j in range(1, nx):
        to = (lax.rem(ix + j, nx), iy)
        second.append(pltpu.make_async_remote_copy(line, lines.at[j], lines_s.at[j], lines_r.at[j], device_id=to, device_id_type=MESH))
        second[-1].start()
    for c in small:
        c.wait()

    for side in range(2):
        order = tables.packed_rows(tables.of_cell((gl.at[side], gt.at[side]), 3 + side, lead))
        pick[side : side + 1, :] = jnp.maximum(order - lead, 0)
    copy = pltpu.make_async_copy(pick, picked, own.at[2])
    copy.start()
    copy.wait()
    load.wait()
    puts = []
    for side in range(2):

        def take(s, _, side=side):
            packed[side, s] = gv[picked[side, s]]
            return 0

        lax.fori_loop(0, per_cell - lead, take, 0)
        for i, room in enumerate(g_rooms):
            puts.append(pltpu.make_async_copy(packed.at[side, pl.ds(0, room)], gp[2 * i + side], put.at[2 * i + side]))
            puts[-1].start()
    keep.wait()
    for c in second:
        c.wait()
    found = jnp.max(lines[...], axis=0)
    lane = lax.broadcasted_iota(I32, found.shape, 1)
    needs = [jnp.max(jnp.where(by_quarter(lane, [int(i == j) for j in range(4)]) == 1, found, 0)) for i in range(4)]
    short = []
    for level_rooms in rooms[:-1]:
        over = [need > room for need, room in zip(needs, level_rooms)]
        short.append(functools.reduce(jnp.logical_or, over).astype(I32))
    level[0, 0] = sum(short)
    for c in large + rest + puts:
        c.wait()


def pack_kernel(f3, z3, f4, z4, z, out3, out4, pick, packed, picked, own, put):
    per_cell, room = z.shape[0], out3.shape[0]
    tables = Tables(per_cell, f3.shape[2])
    for side, lists in enumerate(((f3, z3), (f4, z4))):
        pick[side : side + 1, :] = tables.packed_rows(tables.of_cell(lists, 3 + side))
    copy = pltpu.make_async_copy(pick, picked, own)
    copy.start()
    copy.wait()
    puts = []
    for side, out in enumerate((out3, out4)):

        def take(s, _, side=side):
            packed[side, s] = z[picked[side, s]]
            return 0

        lax.fori_loop(0, room, take, 0)
        puts.append(pltpu.make_async_copy(packed.at[side], out, put.at[side]))
        puts[-1].start()
    for c in puts:
        c.wait()


def plan_kernel(tzg, tfock, tfz, tzgt, t0, t1, t2, t3, t4, f, z, plan, fs, ft, zs, table, cut, put, *, lead):
    per_cell, length = f.shape[0], tfock.shape[2]

    def cut_all(i, _):
        tile = f[i]
        cut[0, i] = split(tile)
        cut[1, i] = split(tile.T)
        cut[2, i] = split(z[i])
        return 0

    lax.fori_loop(0, per_cell, cut_all, 0)
    puts = [pltpu.make_async_copy(cut.at[i], out, put.at[i]) for i, out in enumerate((fs, ft, zs))]
    for c in puts:
        c.start()
    tables = Tables(per_cell, length)
    lane = tables.lane
    plan[...] = jnp.zeros_like(plan)
    for at, tasks, lists, first in (
        (FOCK_ROW, tfock, (tfock, tfz), 0),
        (FZ_ROW, tfz, (tfock, tfz), 0),
        (ZG_ROW, tzg, (tzg, tzgt), lead),
        (ZGT_ROW, tzgt, (tzg, tzgt), lead),
    ):
        plan[at : at + 1, pl.ds(0, length)] = tables.places(tasks, lists, first)
    for k in range(1, 5):
        plan[MAP_ROW + k - 1 : MAP_ROW + k, :] = tables.packed_rows(tables.named((tables.outs(t0, k),)))
    square = (length, length)
    before = (lax.broadcasted_iota(I32, square, 0) < lax.broadcasted_iota(I32, square, 1)).astype(F32)
    same = (lax.broadcasted_iota(I32, square, 0) == lax.broadcasted_iota(I32, square, 1)).astype(F32)
    slots = lax.broadcasted_iota(I32, (length, TILE), 1).astype(F32)
    table[...] = jnp.zeros_like(table)
    for k, tasks in enumerate((t0, t1, t2, t3, t4)):
        here, out = tables.inside(tasks, k), tables.outs(tasks, k)
        slot = out if k == 0 else tables.rank_of(out, tables.named((out,)))
        for i, value in enumerate((slot, tasks[1] - k * per_cell, tasks[2] - k * per_cell, here)):
            table[i : i + 1, :] = value.astype(F32)
        earlier = jnp.dot(table[...], before, preferred_element_type=F32)
        table[4:5, :] = earlier[3:4, :]
        turned = lax.dot_general(same, table[...], (((1,), (1,)), ((), ())), preferred_element_type=F32)
        to_slot = jnp.logical_and(jnp.broadcast_to(turned[:, 4:5], slots.shape) == slots, jnp.broadcast_to(turned[:, 3:4], slots.shape) > 0.5)
        moved = jnp.dot(table[...], to_slot.astype(F32), preferred_element_type=F32).astype(I32)
        count = jnp.sum(here.astype(I32))
        at = LIST_ROW + 4 * k
        for i in range(3):
            plan[at + i : at + i + 1, :] = moved[i : i + 1, :]
        plan[at : at + 1, :] = jnp.where(lane < count, moved[0:1, :], TILE - 1)
        plan[at + 3 : at + 4, :] = jnp.where(lane == TILE - 1, count, 0)
    for c in puts:
        c.wait()


def w_kernel(tasks, plan, zs, g0, g1, g2, a3, g3, a4, g4, ws, grown, cut, total, sems, osem):
    per_cell, lead = zs.shape[0], a3.shape[0]
    copies = fetch(g_places(per_cell, lead, g0, g1, g2, a3, g3, a4, g4), grown, sems)
    total[...] = jnp.zeros_like(total)
    live = live_count(tasks, per_cell)
    for c in copies:
        c.wait()
    entry = moved_entry(tasks, plan, ZG_ROW)
    run_list(live, entry, lambda a: zs[a], lambda b: split(grown[b]), False, total, 4)
    split_all(total, cut, per_cell)
    out = pltpu.make_async_copy(cut, ws, osem)
    out.start()
    out.wait()


def g_places(per_cell, lead, g0, g1, g2, a3, g3, a4, g4):
    places = [(src, k * per_cell) for k, src in enumerate((g0, g1, g2, a3, a4))]
    return places + [(g3, 3 * per_cell + lead), (g4, 4 * per_cell + lead)]


def p_kernel(plan, ft, ws, p0, p1, p2, p3, p4, total, osem):
    outs = (p0, p1, p2, p3, p4)
    starts = [sum(p.shape[0] for p in outs[:k]) for k in range(6)]
    last = starts[5]

    def zero(i, _):
        total[i] = jnp.zeros_like(total[i])
        return 0

    lax.fori_loop(0, last, zero, 0)

    def one(k, _):
        at = LIST_ROW + 4 * k
        first = sum(jnp.where(k == i, start, 0) for i, start in enumerate(starts[:5]))

        def entry(e):
            return jnp.minimum(first + plan[at, e], last), plan[at + 1, e], plan[at + 2, e]

        run_list(plan[at + 3, TILE - 1], entry, lambda a: ft[a], lambda b: ws[b], False, total, 4)
        return 0

    lax.fori_loop(0, 5, one, 0)
    copies = [pltpu.make_async_copy(total.at[pl.ds(starts[k], p.shape[0])], p, osem.at[k]) for k, p in enumerate(outs)]
    for c in copies:
        c.start()
    for c in copies:
        c.wait()


def add_packed(plan, side, packed, total):
    at = MAP_ROW + side

    def add(s, _):
        total[plan[at, s]] += packed[s]
        return 0

    lax.fori_loop(0, jnp.minimum(plan[at, TILE - 1], packed.shape[0]), add, 0)


def rest_kernel(tfock, tfz, tzgt, plan, fs, ws, p0, p1, p2, z0, z1, z2, z3, z4, g0, g1, g2, a3, g3, a4, g4, fock, factor, zgrown, ggrown, us, total, zsem, gsem, osem):
    per_cell, lead = p0.shape[0], a3.shape[0]
    zcopies = fetch([(src, k * per_cell) for k, src in enumerate((z0, z1, z2, z3, z4))], zgrown, zsem)
    gcopies = fetch(g_places(per_cell, lead, g0, g1, g2, a3, g3, a4, g4), ggrown, gsem)
    total[0] = jnp.zeros_like(total[0])
    total[1] = jnp.zeros_like(total[1])
    total[2, pl.ds(0, per_cell)] = p0[...]
    add_packed(plan, 0, p1, total.at[2])
    add_packed(plan, 1, p2, total.at[2])
    fz_live, fock_live, zgt_live = (live_count(tasks, per_cell) for tasks in (tfz, tfock, tzgt))
    for c in zcopies:
        c.wait()
    run_list(fz_live, moved_entry(tfz, plan, FZ_ROW), lambda a: fs[a], lambda b: split(zgrown[b]), False, total.at[0])
    split_all(total.at[0], us, per_cell)
    run_list(fock_live, moved_entry(tfock, plan, FOCK_ROW), lambda a: ws[a], lambda b: split(zgrown[b]), True, total.at[1])
    out1 = pltpu.make_async_copy(total.at[1, pl.ds(0, per_cell)], fock, osem.at[0])
    out1.start()
    for c in gcopies:
        c.wait()
    run_list(zgt_live, moved_entry(tzgt, plan, ZGT_ROW), lambda a: us[a], lambda b: split(ggrown[b]), True, total.at[2])
    out2 = pltpu.make_async_copy(total.at[2, pl.ds(0, per_cell)], factor, osem.at[1])
    out2.start()
    out1.wait()
    out2.wait()


def join_kernel(plan, part, pa, pb, factor, total, puts, *, sides, pieces):
    per_cell = part.shape[0]
    size = per_cell // pieces
    lists = tuple(zip(sides, (pa, pb)))
    counts = [jnp.minimum(plan[MAP_ROW + side, TILE - 1], p.shape[0]) for side, p in lists]
    at = [jnp.int32(0), jnp.int32(0)]
    stored = []
    for i in range(pieces):
        piece = pl.ds(i * size, size)
        total[piece] = part[piece]
        for j, (side, p) in enumerate(lists):

            def more(s, j=j, side=side, i=i):
                return jnp.logical_and(s < counts[j], plan[MAP_ROW + side, s] < (i + 1) * size)

            def add(s, side=side, p=p):
                total[plan[MAP_ROW + side, s]] += p[s]
                return s + 1

            at[j] = lax.while_loop(more, add, at[j])
        stored.append(pltpu.make_async_copy(total.at[piece], factor.at[piece], puts.at[i]))
        stored[-1].start()
    for c in stored:
        c.wait()


SMEM = pl.BlockSpec(memory_space=pltpu.SMEM)
VMEM = pl.BlockSpec(memory_space=pltpu.VMEM)
ANY = pl.BlockSpec(memory_space=pl.ANY)
HBM = pl.BlockSpec(memory_space=pltpu.HBM)
DMA = pltpu.SemaphoreType.DMA


def cost(tasks, tiles):
    return pl.CostEstimate(flops=tasks * 2 * TILE**3 * 8, bytes_accessed=tiles * TILE * TILE * 4, transcendentals=0)


def shifted(array, axis, by):
    n = lax.axis_size(axis)
    return lax.ppermute(array, axis, [(i, (i + by) % n) for i in range(n)])


def tiles(n):
    return jax.ShapeDtypeStruct((n, TILE, TILE), F32)


def cut_tiles(n):
    return jax.ShapeDtypeStruct((n, TILE, 2 * TILE), jnp.bfloat16)


def join(plan, part, pa, pb, sides):
    per_cell = part.shape[0]
    pieces = 4 if per_cell % 4 == 0 else 1
    return pl.pallas_call(
        functools.partial(join_kernel, sides=sides, pieces=pieces),
        name="join_kernel",
        out_shape=pltpu.HBM((per_cell, TILE, TILE), F32),
        in_specs=[SMEM, VMEM, VMEM, VMEM],
        out_specs=HBM,
        scratch_shapes=[pltpu.VMEM((per_cell, TILE, TILE), F32), DMA((pieces,))],
        compiler_params=pltpu.CompilerParams(vmem_limit_bytes=16 * 2**20),
        cost_estimate=cost(0, 4 * per_cell),
    )(plan, part, pa, pb)


def finish(z_room, x_room, y_room, gp3, gp4, z, f, g, tzg, tfock, tfz, tzgt, ttrans, tn, fn, zl, ga):
    per_cell = z.shape[0]
    cap = tzg.shape[2]
    grown = pltpu.VMEM((5 * per_cell, TILE, TILE), F32)
    cut = pltpu.VMEM((per_cell, TILE, 2 * TILE), jnp.bfloat16)
    params = pltpu.CompilerParams(vmem_limit_bytes=40 * 2**20)
    gy = (shifted(gp3, "gy", 1), shifted(gp4, "gy", -1))
    pack = pl.pallas_call(
        pack_kernel,
        name="pack_kernel",
        out_shape=[tiles(z_room)] * 2,
        in_specs=[VMEM] * 5,
        out_specs=[ANY] * 2,
        scratch_shapes=[
            pltpu.VMEM((8, TILE), I32),
            pltpu.VMEM((2, z_room, TILE, TILE), F32),
            pltpu.SMEM((8, TILE), I32),
            DMA,
            DMA((2,)),
        ],
        compiler_params=pltpu.CompilerParams(vmem_limit_bytes=16 * 2**20),
        cost_estimate=cost(0, 4 * per_cell),
    )
    z3, z4 = pack(fn[0], zl[0], fn[1], zl[1], z)
    g_late, z_late, z3, z4 = lax.optimization_barrier((g, z, z3, z4))
    gn = (shifted(g_late, "gx", 1), shifted(g_late, "gx", -1), ga[0], gy[0], ga[1], gy[1])
    zn = (shifted(z_late, "gx", 1), shifted(z_late, "gx", -1), shifted(z3, "gy", 1), shifted(z4, "gy", -1))
    plan, fs, ft, zs = pl.pallas_call(
        functools.partial(plan_kernel, lead=ga[0].shape[0]),
        name="plan_kernel",
        out_shape=[jax.ShapeDtypeStruct((PLAN_ROWS, TILE), I32)] + [cut_tiles(per_cell)] * 3,
        in_specs=[VMEM] * 11,
        out_specs=[VMEM] + [ANY] * 3,
        scratch_shapes=[pltpu.VMEM((8, cap), F32), pltpu.VMEM((3, per_cell, TILE, 2 * TILE), jnp.bfloat16), DMA((3,))],
        compiler_params=pltpu.CompilerParams(vmem_limit_bytes=24 * 2**20),
        cost_estimate=cost(cap, 8 * per_cell),
    )(tzg, tfock, tfz, tzgt, ttrans, *tn, f, z)
    ws = pl.pallas_call(
        w_kernel,
        name="w_kernel",
        out_shape=cut_tiles(per_cell),
        in_specs=[SMEM, SMEM, VMEM] + [ANY] * 7,
        out_specs=ANY,
        scratch_shapes=[grown, cut, pltpu.VMEM((per_cell + 1, TILE, TILE), F32), DMA((7,)), DMA],
        compiler_params=params,
        cost_estimate=cost(cap, 7 * per_cell),
    )(tzg, plan, zs, g, *gn)
    p = pl.pallas_call(
        p_kernel,
        name="p_kernel",
        out_shape=[tiles(n) for n in (per_cell, x_room, x_room, y_room, y_room)],
        in_specs=[SMEM] + [VMEM] * 2,
        out_specs=[ANY] * 5,
        scratch_shapes=[pltpu.VMEM((per_cell + 2 * x_room + 2 * y_room + 1, TILE, TILE), F32), DMA((5,))],
        compiler_params=params,
        cost_estimate=cost(2 * cap, 7 * per_cell),
    )(plan, ft, ws)
    pn = [shifted(p[k + 1], axis, -by) for k, (axis, by) in enumerate(STEPS)]
    fock_grad, part = pl.pallas_call(
        rest_kernel,
        name="rest_kernel",
        out_shape=[pltpu.HBM((per_cell, TILE, TILE), F32), tiles(per_cell)],
        in_specs=[SMEM] * 4 + [VMEM] * 5 + [ANY] * 12,
        out_specs=[HBM, ANY],
        scratch_shapes=[grown, grown, cut, pltpu.VMEM((3, per_cell + 1, TILE, TILE), F32), DMA((5,)), DMA((7,)), DMA((2,))],
        compiler_params=params,
        cost_estimate=cost(3 * cap, 14 * per_cell),
    )(tfock, tfz, tzgt, plan, fs, ws, p[0], pn[0], pn[1], z, *zn, g, *gn)
    return fock_grad, join(plan, part, pn[2], pn[3], (2, 3))


def rooms_of(per_cell, lead):
    levels = ((13, 18, 15, 12), (13, 19, 15, 13), (14, 20, 16, 14), (15, 21, 18, 16))
    scaled = [tuple(per_cell * room // 24 for room in level) for level in levels]
    return scaled + [(per_cell - lead,) + (per_cell,) * 3]


def body(z_factor, fock, cotangent, tasks_zg, tasks_fock, tasks_fz, tasks_zgt, tasks_trans):
    per_cell = z_factor.shape[2]
    nx, ny = lax.axis_size("gx"), lax.axis_size("gy")
    z, f, g = z_factor[0, 0], fock[0, 0], cotangent[0, 0]
    lists = (tasks_zg, tasks_fock, tasks_fz, tasks_zgt, tasks_trans)
    tzg, tfock, tfz, tzgt, ttrans = (t.reshape(t.shape[2], 1, t.shape[3]) for t in lists)
    a_list = jax.ShapeDtypeStruct(tzg.shape, I32)
    lead = per_cell // 3
    rooms = rooms_of(per_cell, lead)
    g_rooms = sorted({room[0] for room in rooms})
    packs = 2 * len(g_rooms)
    met = pl.pallas_call(
        functools.partial(meet_kernel, rooms=rooms, g_rooms=g_rooms, lead=lead, cuts=lead // 4),
        name="meet_kernel",
        out_shape=[tiles(lead)] * 2 + [a_list] * 8 + [tiles(room) for room in g_rooms for _ in range(2)] + [jax.ShapeDtypeStruct((1, 1), I32)],
        in_specs=[VMEM] * 5 + [ANY],
        out_specs=[ANY] * 2 + [VMEM] * 8 + [ANY] * packs + [SMEM],
        scratch_shapes=[
            pltpu.VMEM((2,) + tzg.shape, I32),
            pltpu.VMEM((2,) + tzg.shape, I32),
            pltpu.VMEM((1, TILE), I32),
            pltpu.VMEM((ny, TILE), I32),
            pltpu.VMEM((nx, ny, TILE), I32),
            pltpu.VMEM((8, TILE), I32),
            pltpu.SMEM((8, TILE), I32),
            pltpu.VMEM((per_cell - lead, TILE, TILE), F32),
            pltpu.VMEM((2, per_cell - lead, TILE, TILE), F32),
            DMA((4,)),
            DMA((4,)),
            DMA((12,)),
            DMA((12,)),
            DMA((ny,)),
            DMA((ny,)),
            DMA((nx,)),
            DMA((nx,)),
            DMA((4,)),
            DMA((packs,)),
        ],
        compiler_params=pltpu.CompilerParams(collective_id=0, has_side_effects=True),
    )(tzg, tfock, tfz, tzgt, ttrans, g)
    ga, tn, fn, zl, gp, level = met[:2], met[2:6], met[6:8], met[8:10], met[10 : 10 + packs], met[-1]

    def branch(g_room, z_room, x_room, y_room):
        at = 2 * g_rooms.index(g_room)
        return lambda gp, *rest: finish(z_room, x_room, y_room, gp[at], gp[at + 1], *rest)

    operands = (gp, z, f, g, tzg, tfock, tfz, tzgt, ttrans, tn, fn, zl, ga)
    fock_grad, factor_grad = lax.switch(level[0, 0], [branch(*room) for room in rooms], *operands)
    return fock_grad[None, None], factor_grad[None, None]


def solution(mesh):
    cells = P("gx", "gy", None, None, None)
    lists = P("gx", "gy", None, None)
    return jax.shard_map(
        body,
        mesh=mesh,
        in_specs=(cells,) * 3 + (lists,) * 5,
        out_specs=(cells, cells),
        check_vma=False,
    )
```

profile of v0, /device:TPU:0, one launch (start us, length us, event | category | flops | bytes accessed | tf_op | source)
XLA Modules:
  0.0 121.6 jit_solution(16025300701737558086)
XLA Ops:
  0.7 24.5 %meet_kernel.1 = (f32[8,128,128]{2,1,0:T(8,128)S(1)}, f32[8,128,128]{2,1,0:T(8,128)S(1)}, s32[3,1,64]{2,1,0:T(1,128)S(1)}, s32[3,1,64]{2,1,0:T(1,128)S(1)}, s32[...) custom-call(s32[3,1,64]{2,1,0:T(1,128)} %bitcast.20, ...), custom_call_target="tpu_custom_call" | custom-call | tf_op jit(solution)/shard_map/meet_kernel/pallas_call | solution.py:559
  25.8 95.6 %conditional.1 = (f32[24,128,128]{2,1,0:T(8,128)}, f32[1,1,24,128,128]{4,3,2,1,0:T(8,128)}) conditional(s32[]{:T(128)} %bitcast.11, (s32[3,1,64]{2,1,0:T(1,128)S(1)}, s32[3,1,64]{2,1,0:T(1,128)S(1)}, s32[3,1,64]{2,1,0:T(1,128)S(1)}, s32[3,1,64]{2,1,0:T(1,128)S(1)}, s32[3,1,64]{2,1,0:T(1,128)S(1)}, ...), branch_computations={%region_0.0_spmd, %region_1.0_spmd, %region_2.0_spmd, %region_3.0_... | conditional | flops 15032385536 | bytes 195035856 | solution.py:595
  26.0 0.0 copy-start.20
  26.1 3.1 %pack_kernel.7 = (f32[20,128,128]{2,1,0:T(8,128)S(1)}, f32[20,128,128]{2,1,0:T(8,128)S(1)}) custom-call(s32[3,1,64]{2,1,0:T(1,128)S(1)} %get-tuple-element.290.f3, s32[3,1,64]{2,1,0:T(1,128)S(1)} %get-tuple-element.291.z3, s32[3,1,64]{2,1,0:T(1,128)S(1)} %get-tuple-element.292.f4, s32[3,1,64]{2,1,0:T(1,128)S(1)} %get-tuple-element.293.z4, ...), custom_call_target="tpu_custom_call" | custom-call | bytes 6291456 | tf_op jit(solution)/shard_map/cond/branch_2_fun/pack_kernel/pallas_call | solution.py:494
  29.2 0.1 collective-permute-start.25
  29.3 0.4 collective-permute-start.24
  29.7 5.3 %collective-permute-start.27 = (f32[14,128,128]{2,1,0:T(8,128)}, f32[14,128,128]{2,1,0:T(8,128)S(1)}, u32[]{:S(2)}, u32[]{:S(2)}) collective-permute-start(f32[14,128,128]{2,1,0:T(8,128)} %get-tuple-element.300), channel_id=1, source_target_pairs={{0,15},{1,0},{2,1},{3,2},{4,3},{5,4},{6,5},{7,6},{8,7},{9,8},{10,9... | collective-permute-start | bytes 2752520 | tf_op jit(solution)/shard_map/cond/branch_2_fun/ppermute | solution.py:445
  35.1 21.2 %collective-permute-done.26.g3 = f32[14,128,128]{2,1,0:T(8,128)S(1)} collective-permute-done((f32[14,128,128]{2,1,0:T(8,128)S(1)}, f32[14,128,128]{2,1,0:T(8,128)S(1)}, u32[]{:S(2)}, u32[]{:S(2)}) %collective-permute-start.26) | collective-permute-done | bytes 917536 | tf_op jit(solution)/shard_map/cond/branch_2_fun/ppermute | solution.py:445
  56.3 1.7 %collective-permute-start.31 = (f32[24,128,128]{2,1,0:T(8,128)}, f32[24,128,128]{2,1,0:T(8,128)}, u32[]{:S(2)}, u32[]{:S(2)}) collective-permute-start(f32[24,128,128]{2,1,0:T(8,128)} %get-tuple-element.305.z.z0), channel_id=1, source_target_pairs={{0,112},{16,0},{32,16},{48,32},{64,48},{80,64},{96,80},{112,96},{1... | collective-permute-start | bytes 4718600 | tf_op jit(solution)/shard_map/cond/branch_2_fun/ppermute | solution.py:445
  58.0 5.9 %plan_kernel.7 = (s32[32,128]{1,0:T(8,128)S(1)}, bf16[24,128,256]{2,1,0:T(8,128)(2,1)S(1)}, bf16[24,128,256]{2,1,0:T(8,128)(2,1)S(1)}, bf16[24,128,256]{2,1,0:T(8,128)(2,1)S(1)}) custom-call(s32[3,1,64]{2,1,0:T(1,128)S(1)} %get-tuple-element.278.tzg.tasks, s32[3,1,64]{2,1,0:T(1,128)S(1)} %get-tuple-element.275.tfock, ...), custom_call_target="tpu_custom_call" | custom-call | flops 2147483648 | bytes 12582912 | tf_op jit(solution)/shard_map/cond/branch_2_fun/plan_kernel/pallas_call | solution.py:498
  63.9 0.0 collective-permute-start.30
  63.9 0.2 collective-permute-start.33
  64.1 5.3 %w_kernel.7.ws = bf16[24,128,256]{2,1,0:T(8,128)(2,1)S(1)} custom-call(s32[3,1,64]{2,1,0:T(1,128)S(1)} %get-tuple-element.278.tzg.tasks, s32[32,128]{1,0:T(8,128)S(1)} %get-tuple-element.286.plan, bf16[24,128,256]{2,1,0:T(8,128)(2,1)S(1)} %get-tuple-element.288.zs, f32[24,128,128]{2,1,0:T(8,128)} %get-tuple-element.296.g0, ...), custom_call_target="tpu_custom_call" | custom-call | flops 2147483648 | bytes 11010048 | tf_op jit(solution)/shard_map/cond/branch_2_fun/w_kernel/pallas_call | solution.py:508
  69.5 4.4 %p_kernel.7 = (f32[24,128,128]{2,1,0:T(8,128)S(1)}, f32[16,128,128]{2,1,0:T(8,128)S(1)}, f32[16,128,128]{2,1,0:T(8,128)S(1)}, f32[14,128,128]{2,1,0:T(8,128)S(1)}, f32[14,128,128]{2,1,0:T(8,128)S(1)}) custom-call(s32[32,128]{1,0:T(8,128)S(1)} %get-tuple-element.286.plan, bf16[24,128,256]{2,1,0:T(8,128)(2,1)S(1)} %get-tuple-element.301.ft, ...), custom_call_target="tpu_custom_call" | custom-call | flops 4294967296 | bytes 11010048 | tf_op jit(solution)/shard_map/cond/branch_2_fun/p_kernel/pallas_call | solution.py:518
  73.9 0.0 copy-start.16
  73.9 1.1 copy-done.16
  75.0 9.2 %collective-permute-done.32.z3 = f32[20,128,128]{2,1,0:T(8,128)S(1)} collective-permute-done((f32[20,128,128]{2,1,0:T(8,128)S(1)}, f32[20,128,128]{2,1,0:T(8,128)S(1)}, u32[]{:S(2)}, u32[]{:S(2)}) %collective-permute-start.32) | collective-permute-done | bytes 1310752 | tf_op jit(solution)/shard_map/cond/branch_2_fun/ppermute | solution.py:445
  84.3 0.6 collective-permute-start.29
  84.9 9.7 %collective-permute-done.33.z4 = f32[20,128,128]{2,1,0:T(8,128)S(1)} collective-permute-done((f32[20,128,128]{2,1,0:T(8,128)S(1)}, f32[20,128,128]{2,1,0:T(8,128)S(1)}, u32[]{:S(2)}, u32[]{:S(2)}) %collective-permute-start.33) | collective-permute-done | bytes 1310752 | tf_op jit(solution)/shard_map/cond/branch_2_fun/ppermute | solution.py:445
  94.5 5.3 %collective-permute-start.35 = (f32[14,128,128]{2,1,0:T(8,128)S(1)}, f32[14,128,128]{2,1,0:T(8,128)S(1)}, u32[]{:S(2)}, u32[]{:S(2)}) collective-permute-start(f32[14,128,128]{2,1,0:T(8,128)S(1)} %get-tuple-element.311), channel_id=1, source_target_pairs={{0,15},{1,0},{2,1},{3,2},{4,3},{5,4},{6,5},{7,6},{8,7},{9,8},{10,9... | collective-permute-start | bytes 2752520 | tf_op jit(solution)/shard_map/cond/branch_2_fun/ppermute | solution.py:445
  99.9 1.4 %copy-done.17 = f32[24,128,128]{2,1,0:T(8,128)S(1)} copy-done((f32[24,128,128]{2,1,0:T(8,128)S(1)}, f32[24,128,128]{2,1,0:T(8,128)}, u32[]{:S(2)}) %copy-start.17) | copy-done | bytes 1572888 | tf_op jit(solution)/shard_map/cond
  101.3 10.7 %rest_kernel.7 = (f32[24,128,128]{2,1,0:T(8,128)}, f32[24,128,128]{2,1,0:T(8,128)S(1)}) custom-call(s32[3,1,64]{2,1,0:T(1,128)S(1)} %get-tuple-element.275.tfock, s32[3,1,64]{2,1,0:T(1,128)S(1)} %get-tuple-element.276.tfz, s32[3,1,64]{2,1,0:T(1,128)S(1)} %get-tuple-element.277.tzgt, s32[32,128]{1,0:T(8,128)S(1)} %get-tuple-element.286.plan, ...), custom_call_target="tpu_custom_call" | custom-call | flops 6442450944 | bytes 22020096 | tf_op jit(solution)/shard_map/cond/branch_2_fun/rest_kernel/pallas_call | solution.py:529
  112.0 7.1 %collective-permute-done.34.pa = f32[14,128,128]{2,1,0:T(8,128)S(1)} collective-permute-done((f32[14,128,128]{2,1,0:T(8,128)S(1)}, f32[14,128,128]{2,1,0:T(8,128)S(1)}, u32[]{:S(2)}, u32[]{:S(2)}) %collective-permute-start.34) | collective-permute-done | bytes 917536 | tf_op jit(solution)/shard_map/cond/branch_2_fun/ppermute | solution.py:445
  119.1 2.1 %join_kernel.7 = f32[24,128,128]{2,1,0:T(8,128)} custom-call(s32[32,128]{1,0:T(8,128)S(1)} %get-tuple-element.286.plan, f32[24,128,128]{2,1,0:T(8,128)S(1)} %get-tuple-element.309.part, f32[14,128,128]{2,1,0:T(8,128)S(1)} %collective-permute-done.34.pa, f32[14,128,128]{2,1,0:T(8,128)S(1)} %collective-permute-done.35.pb), custom_call_target="tpu_custom_call" | custom-call | bytes 6291456 | tf_op jit(solution)/shard_map/cond/branch_2_fun/join_kernel/pallas_call | solution.py:459
  (36 shorter events, 0.1 us)
Async XLA Ops:
  0.6 25.1 %copy-start.30 = (s32[1,1,3,64]{3,1,2,0:T(1,128)S(1)}, s32[1,1,3,64]{3,1,2,0:T(1,128)}, u32[]{:S(2)}) copy-start(s32[1,1,3,64]{3,1,2,0:T(1,128)} %param.20) | copy-start | bytes 2308
  0.6 25.1 %copy-start.29 = (s32[1,1,3,64]{3,1,2,0:T(1,128)S(1)}, s32[1,1,3,64]{3,1,2,0:T(1,128)}, u32[]{:S(2)}) copy-start(s32[1,1,3,64]{3,1,2,0:T(1,128)} %param.19) | copy-start | bytes 2308
  0.7 25.1 %copy-start.28 = (s32[1,1,3,64]{3,1,2,0:T(1,128)S(1)}, s32[1,1,3,64]{3,1,2,0:T(1,128)}, u32[]{:S(2)}) copy-start(s32[1,1,3,64]{3,1,2,0:T(1,128)} %param.18) | copy-start | bytes 2308
  0.7 25.1 %copy-start.27 = (s32[1,1,3,64]{3,1,2,0:T(1,128)S(1)}, s32[1,1,3,64]{3,1,2,0:T(1,128)}, u32[]{:S(2)}) copy-start(s32[1,1,3,64]{3,1,2,0:T(1,128)} %param.17) | copy-start | bytes 2308
  0.7 25.1 %copy-start.26 = (s32[1,1,3,64]{3,1,2,0:T(1,128)S(1)}, s32[1,1,3,64]{3,1,2,0:T(1,128)}, u32[]{:S(2)}) copy-start(s32[1,1,3,64]{3,1,2,0:T(1,128)} %param.16) | copy-start | bytes 2308
  0.7 25.1 %copy-start.31 = (f32[1,1,24,128,128]{4,3,2,1,0:T(8,128)S(1)}, f32[1,1,24,128,128]{4,3,2,1,0:T(8,128)}, u32[]{:S(2)}) copy-start(f32[1,1,24,128,128]{4,3,2,1,0:T(8,128)} %param.14) | copy-start | bytes 4718596
  26.0 31.9 %copy-start.20 = (f32[8,128,128]{2,1,0:T(8,128)}, f32[8,128,128]{2,1,0:T(8,128)S(1)}, u32[]{:S(2)}) copy-start(f32[8,128,128]{2,1,0:T(8,128)S(1)} %get-tuple-element.299.a4) | copy-start | bytes 1572868 | tf_op jit(solution)/shard_map/cond
  26.0 3.7 %copy-start.39 = (f32[14,128,128]{2,1,0:T(8,128)S(1)}, f32[14,128,128]{2,1,0:T(8,128)}, u32[]{:S(2)}) copy-start(f32[14,128,128]{2,1,0:T(8,128)} %get-tuple-element.298) | copy-start | bytes 2752516 | tf_op jit(solution)/shard_map/cond
  29.2 34.7 %collective-permute-start.25 = (f32[24,128,128]{2,1,0:T(8,128)}, f32[24,128,128]{2,1,0:T(8,128)S(1)}, u32[]{:S(2)}, u32[]{:S(2)}) collective-permute-start(f32[24,128,128]{2,1,0:T(8,128)} %get-tuple-element.296.g0), channel_id=1, source_target_pairs={{0,112},{16,0},{32,16},{48,32},{64,48},{80,64},{96,80},{112,96},{1... | collective-permute-start | bytes 4718600 | tf_op jit(solution)/shard_map/cond/branch_2_fun/ppermute | solution.py:445
  29.3 34.8 %collective-permute-start.24 = (f32[24,128,128]{2,1,0:T(8,128)}, f32[24,128,128]{2,1,0:T(8,128)S(1)}, u32[]{:S(2)}, u32[]{:S(2)}) collective-permute-start(f32[24,128,128]{2,1,0:T(8,128)} %get-tuple-element.296.g0), channel_id=1, source_target_pairs={{0,16},{16,32},{32,48},{48,64},{64,80},{80,96},{96,112},{112,0},{1... | collective-permute-start | bytes 4718600 | tf_op jit(solution)/shard_map/cond/branch_2_fun/ppermute | solution.py:445
  29.7 26.5 %collective-permute-start.26 = (f32[14,128,128]{2,1,0:T(8,128)S(1)}, f32[14,128,128]{2,1,0:T(8,128)S(1)}, u32[]{:S(2)}, u32[]{:S(2)}) collective-permute-start(f32[14,128,128]{2,1,0:T(8,128)S(1)} %copy-done.39), channel_id=1, source_target_pairs={{0,1},{1,2},{2,3},{3,4},{4,5},{5,6},{6,7},{7,8},{8,9},{9,10},{10,1... | collective-permute-start | bytes 2752520 | tf_op jit(solution)/shard_map/cond/branch_2_fun/ppermute | solution.py:445
  29.7 34.2 %collective-permute-start.27 = (f32[14,128,128]{2,1,0:T(8,128)}, f32[14,128,128]{2,1,0:T(8,128)S(1)}, u32[]{:S(2)}, u32[]{:S(2)}) collective-permute-start(f32[14,128,128]{2,1,0:T(8,128)} %get-tuple-element.300), channel_id=1, source_target_pairs={{0,15},{1,0},{2,1},{3,2},{4,3},{5,4},{6,5},{7,6},{8,7},{9,8},{10,9... | collective-permute-start | bytes 2752520 | tf_op jit(solution)/shard_map/cond/branch_2_fun/ppermute | solution.py:445
  35.1 49.2 %collective-permute-start.32 = (f32[20,128,128]{2,1,0:T(8,128)S(1)}, f32[20,128,128]{2,1,0:T(8,128)S(1)}, u32[]{:S(2)}, u32[]{:S(2)}) collective-permute-start(f32[20,128,128]{2,1,0:T(8,128)S(1)} %get-tuple-element.306), channel_id=1, source_target_pairs={{0,1},{1,2},{2,3},{3,4},{4,5},{5,6},{6,7},{7,8},{8,9},{9,10},{10,1... | collective-permute-start | bytes 3932168 | tf_op jit(solution)/shard_map/cond/branch_2_fun/ppermute | solution.py:445
  56.3 38.3 %collective-permute-start.31 = (f32[24,128,128]{2,1,0:T(8,128)}, f32[24,128,128]{2,1,0:T(8,128)}, u32[]{:S(2)}, u32[]{:S(2)}) collective-permute-start(f32[24,128,128]{2,1,0:T(8,128)} %get-tuple-element.305.z.z0), channel_id=1, source_target_pairs={{0,112},{16,0},{32,16},{48,32},{64,48},{80,64},{96,80},{112,96},{1... | collective-permute-start | bytes 4718600 | tf_op jit(solution)/shard_map/cond/branch_2_fun/ppermute | solution.py:445
  58.0 6.1 %copy-start.21 = (f32[8,128,128]{2,1,0:T(8,128)S(1)}, f32[8,128,128]{2,1,0:T(8,128)}, u32[]{:S(2)}) copy-start(f32[8,128,128]{2,1,0:T(8,128)} %copy-done.20) | copy-start | bytes 1572868 | tf_op jit(solution)/shard_map/cond
  63.9 36.0 %collective-permute-start.30 = (f32[24,128,128]{2,1,0:T(8,128)}, f32[24,128,128]{2,1,0:T(8,128)S(1)}, u32[]{:S(2)}, u32[]{:S(2)}) collective-permute-start(f32[24,128,128]{2,1,0:T(8,128)} %get-tuple-element.305.z.z0), channel_id=1, source_target_pairs={{0,16},{16,32},{32,48},{48,64},{64,80},{80,96},{96,112},{112,0},{1... | collective-permute-start | bytes 4718600 | tf_op jit(solution)/shard_map/cond/branch_2_fun/ppermute | solution.py:445
  63.9 5.5 %copy-start.2 = (f32[24,128,128]{2,1,0:T(8,128)}, f32[24,128,128]{2,1,0:T(8,128)S(1)}, u32[]{:S(2)}) copy-start(f32[24,128,128]{2,1,0:T(8,128)S(1)} %collective-permute-done.25.g2) | copy-start | bytes 4718596 | tf_op jit(solution)/shard_map/cond
  63.9 30.6 %collective-permute-start.33 = (f32[20,128,128]{2,1,0:T(8,128)S(1)}, f32[20,128,128]{2,1,0:T(8,128)S(1)}, u32[]{:S(2)}, u32[]{:S(2)}) collective-permute-start(f32[20,128,128]{2,1,0:T(8,128)S(1)} %get-tuple-element.307), channel_id=1, source_target_pairs={{0,15},{1,0},{2,1},{3,2},{4,3},{5,4},{6,5},{7,6},{8,7},{9,8},{10,9... | collective-permute-start | bytes 3932168 | tf_op jit(solution)/shard_map/cond/branch_2_fun/ppermute | solution.py:445
  64.1 5.3 %copy-start.7 = (f32[24,128,128]{2,1,0:T(8,128)}, f32[24,128,128]{2,1,0:T(8,128)S(1)}, u32[]{:S(2)}) copy-start(f32[24,128,128]{2,1,0:T(8,128)S(1)} %collective-permute-done.24.g1) | copy-start | bytes 4718596 | tf_op jit(solution)/shard_map/cond
  69.4 30.5 %copy-start.22 = (f32[8,128,128]{2,1,0:T(8,128)S(1)}, f32[8,128,128]{2,1,0:T(8,128)}, u32[]{:S(2)}) copy-start(f32[8,128,128]{2,1,0:T(8,128)} %copy-done.20) | copy-start | bytes 1572868 | tf_op jit(solution)/shard_map/cond
  75.0 24.9 %collective-permute-start.28 = (f32[16,128,128]{2,1,0:T(8,128)S(1)}, f32[16,128,128]{2,1,0:T(8,128)S(1)}, u32[]{:S(2)}, u32[]{:S(2)}) collective-permute-start(f32[16,128,128]{2,1,0:T(8,128)S(1)} %get-tuple-element.303), channel_id=1, source_target_pairs={{0,16},{16,32},{32,48},{48,64},{64,80},{80,96},{96,112},{112,0},{1... | collective-permute-start | bytes 3145736 | tf_op jit(solution)/shard_map/cond/branch_2_fun/ppermute | solution.py:445
  84.3 15.6 %collective-permute-start.29 = (f32[16,128,128]{2,1,0:T(8,128)S(1)}, f32[16,128,128]{2,1,0:T(8,128)S(1)}, u32[]{:S(2)}, u32[]{:S(2)}) collective-permute-start(f32[16,128,128]{2,1,0:T(8,128)S(1)} %get-tuple-element.304), channel_id=1, source_target_pairs={{0,112},{16,0},{32,16},{48,32},{64,48},{80,64},{96,80},{112,96},{1... | collective-permute-start | bytes 3145736 | tf_op jit(solution)/shard_map/cond/branch_2_fun/ppermute | solution.py:445
  94.5 24.6 %collective-permute-start.34 = (f32[14,128,128]{2,1,0:T(8,128)S(1)}, f32[14,128,128]{2,1,0:T(8,128)S(1)}, u32[]{:S(2)}, u32[]{:S(2)}) collective-permute-start(f32[14,128,128]{2,1,0:T(8,128)S(1)} %get-tuple-element.310), channel_id=1, source_target_pairs={{0,1},{1,2},{2,3},{3,4},{4,5},{5,6},{6,7},{7,8},{8,9},{9,10},{10,1... | collective-permute-start | bytes 2752520 | tf_op jit(solution)/shard_map/cond/branch_2_fun/ppermute | solution.py:445
  94.5 24.6 %collective-permute-start.35 = (f32[14,128,128]{2,1,0:T(8,128)S(1)}, f32[14,128,128]{2,1,0:T(8,128)S(1)}, u32[]{:S(2)}, u32[]{:S(2)}) collective-permute-start(f32[14,128,128]{2,1,0:T(8,128)S(1)} %get-tuple-element.311), channel_id=1, source_target_pairs={{0,15},{1,0},{2,1},{3,2},{4,3},{5,4},{6,5},{7,6},{8,7},{9,8},{10,9... | collective-permute-start | bytes 2752520 | tf_op jit(solution)/shard_map/cond/branch_2_fun/ppermute | solution.py:445
  (2 other events, 2.6 us)
where the time goes:
time: 122 us
  Pallas kernels  56 us (46%)
  waiting for transfers between devices  47.2 us (39%)
  starting transfers between devices  13.7 us (11%)
  local copies, waits for them, and re-layouts  2.59 us (2%)
  between operations  1.54 us (1%)
    ppermute x12, waiting for transfers between devices, shifted(): return lax.ppermute(array, axis, [(i, (i + by) % n) for i in range(n)])  47.2 us
    pallas_call x1, Pallas kernels, body(): pl.pallas_call(functools.partial(meet_kernel, rooms=rooms, g_rooms=g_room...  24.5 us
    ppermute x12, starting transfers between devices, shifted(): return lax.ppermute(array, axis, [(i, (i + by) % n) for i in range(n)])  13.7 us
    pallas_call x1, Pallas kernels, finish(): pl.pallas_call(rest_kernel, name='rest_kernel', out_shape=[pltpu.HBM((per...  10.7 us
    pallas_call x1, Pallas kernels, finish(): pl.pallas_call(functools.partial(plan_kernel, lead=ga[0].shape[0]), name=...  5.9 us
    pallas_call x1, Pallas kernels, finish(): pl.pallas_call(w_kernel, name='w_kernel', out_shape=cut_tiles(per_cell),...  5.31 us
    pallas_call x1, Pallas kernels, finish(): pl.pallas_call(p_kernel, name='p_kernel', out_shape=[tiles(n) for n in (p...  4.42 us
    pallas_call x1, Pallas kernels, finish(): z3, z4 = pack(fn[0], zl[0], fn[1], zl[1], z)  3.15 us
  transfers between devices with their start and end apart: 12, of which 4 were waited for; matrix products, arithmetic and copies ran while one was open for 0% of the time, Pallas kernels for 22%

commit v1 on v0

--- a/solution.py
+++ b/solution.py
@@ -60,6 +60,21 @@
         return 0
 
     lax.fori_loop(0, per_cell, step, 0)
+
+
+def each(count, do):
+    def step(i, _):
+        do(i)
+        return 0
+
+    lax.fori_loop(0, count, step, 0)
+
+
+def clear(total, first, count):
+    def do(i):
+        total[first + i] = jnp.zeros(total.shape[1:], total.dtype)
+
+    each(count, do)
 
 
 def moved_entry(tasks, plan, at):
@@ -156,6 +171,16 @@
         others.append((lax.rem(ix + by + nx, nx), iy) if axis == "gx" else (ix, lax.rem(iy + by + ny, ny)))
     pl.semaphore_wait(barrier, nx + ny - 2)
 
+    def bulk(i, k, start, size):
+        part = pl.ds(start, size)
+        return pltpu.make_async_remote_copy(
+            g.at[part], ga[(k ^ 1) - 2].at[part], bulk_s.at[i], bulk_r.at[i], device_id=others[k], device_id_type=MESH
+        )
+
+    large = [bulk(0, 2, 0, cuts), bulk(1, 3, 0, cuts)]
+    for c in large:
+        c.start()
+
     lists = []
     for i in range(2):
         lists += [(tzg, gl.at[i], others[2 + i]), (tzgt, gt.at[i], others[2 + i])]
@@ -165,16 +190,6 @@
     for i, (src, dst, to) in enumerate(lists):
         small.append(pltpu.make_async_remote_copy(src, dst, list_s.at[i], list_r.at[i], device_id=to, device_id_type=MESH))
         small[-1].start()
-
-    def bulk(i, k, start, size):
-        part = pl.ds(start, size)
-        return pltpu.make_async_remote_copy(
-            g.at[part], ga[(k ^ 1) - 2].at[part], bulk_s.at[i], bulk_r.at[i], device_id=others[k], device_id_type=MESH
-        )
-
-    large = [bulk(0, 2, 0, cuts), bulk(1, 3, 0, cuts)]
-    for c in large:
-        c.start()
 
     tables = Tables(per_cell, tfock.shape[2])
 
@@ -236,11 +251,12 @@
     found = jnp.max(lines[...], axis=0)
     lane = lax.broadcasted_iota(I32, found.shape, 1)
     needs = [jnp.max(jnp.where(by_quarter(lane, [int(i == j) for j in range(4)]) == 1, found, 0)) for i in range(4)]
-    short = []
+    first_fit, unfit = 0, jnp.int32(1)
     for level_rooms in rooms[:-1]:
         over = [need > room for need, room in zip(needs, level_rooms)]
-        short.append(functools.reduce(jnp.logical_or, over).astype(I32))
-    level[0, 0] = sum(short)
+        unfit = unfit * functools.reduce(jnp.logical_or, over).astype(I32)
+        first_fit = first_fit + unfit
+    level[0, 0] = first_fit
     for c in large + rest + puts:
         c.wait()
 
@@ -321,7 +337,7 @@
 def w_kernel(tasks, plan, zs, g0, g1, g2, a3, g3, a4, g4, ws, grown, cut, total, sems, osem):
     per_cell, lead = zs.shape[0], a3.shape[0]
     copies = fetch(g_places(per_cell, lead, g0, g1, g2, a3, g3, a4, g4), grown, sems)
-    total[...] = jnp.zeros_like(total)
+    clear(total, 0, per_cell)
     live = live_count(tasks, per_cell)
     for c in copies:
         c.wait()
@@ -343,11 +359,7 @@
     starts = [sum(p.shape[0] for p in outs[:k]) for k in range(6)]
     last = starts[5]
 
-    def zero(i, _):
-        total[i] = jnp.zeros_like(total[i])
-        return 0
-
-    lax.fori_loop(0, last, zero, 0)
+    clear(total, 0, last)
 
     def one(k, _):
         at = LIST_ROW + 4 * k
@@ -381,9 +393,13 @@
     per_cell, lead = p0.shape[0], a3.shape[0]
     zcopies = fetch([(src, k * per_cell) for k, src in enumerate((z0, z1, z2, z3, z4))], zgrown, zsem)
     gcopies = fetch(g_places(per_cell, lead, g0, g1, g2, a3, g3, a4, g4), ggrown, gsem)
-    total[0] = jnp.zeros_like(total[0])
-    total[1] = jnp.zeros_like(total[1])
-    total[2, pl.ds(0, per_cell)] = p0[...]
+    clear(total.at[0], 0, per_cell)
+    clear(total.at[1], 0, per_cell)
+
+    def begin(i):
+        total[2, i] = p0[i]
+
+    each(per_cell, begin)
     add_packed(plan, 0, p1, total.at[2])
     add_packed(plan, 1, p2, total.at[2])
     fz_live, fock_live, zgt_live = (live_count(tasks, per_cell) for tasks in (tfz, tfock, tzgt))
@@ -412,7 +428,11 @@
     stored = []
     for i in range(pieces):
         piece = pl.ds(i * size, size)
-        total[piece] = part[piece]
+
+        def begin(t, i=i):
+            total[i * size + t] = part[i * size + t]
+
+        each(size, begin)
         for j, (side, p) in enumerate(lists):
 
             def more(s, j=j, side=side, i=i):
@@ -540,7 +560,7 @@
 
 
 def rooms_of(per_cell, lead):
-    levels = ((13, 18, 15, 12), (13, 19, 15, 13), (14, 20, 16, 14), (15, 21, 18, 16))
+    levels = ((13, 18, 18, 12), (14, 18, 18, 13), (13, 19, 18, 14), (14, 20, 18, 15), (16, 22, 18, 17))
     scaled = [tuple(per_cell * room // 24 for room in level) for level in levels]
     return scaled + [(per_cell - lead,) + (per_cell,) * 3]
 

time: 122 us -> 123 us (level)
  waiting for transfers between devices: 47.2 us -> 49.1 us
  local copies, waits for them, and re-layouts: 2.59 us -> 1.16 us
    ppermute x12, waiting for transfers between devices: 47.2 us -> 49.1 us  [shifted(): return lax.ppermute(array, axis, [(i, (i + by) % n) for i in range(n)])]
    cond x16 -> x10, local copies, waits for them, and re-layouts: 2.57 us -> 1.13 us
where the time goes in v1:
time: 123 us
  Pallas kernels  56.6 us (46%)
  waiting for transfers between devices  49.1 us (40%)
  starting transfers between devices  13.7 us (11%)
  between operations  1.58 us (1%)
    ppermute x12, waiting for transfers between devices, shifted(): return lax.ppermute(array, axis, [(i, (i + by) % n) for i in range(n)])  49.1 us
    pallas_call x1, Pallas kernels, body(): pl.pallas_call(functools.partial(meet_kernel, rooms=rooms, g_rooms=g_room...  24.5 us
    ppermute x12, starting transfers between devices, shifted(): return lax.ppermute(array, axis, [(i, (i + by) % n) for i in range(n)])  13.7 us
    pallas_call x1, Pallas kernels, finish(): pl.pallas_call(rest_kernel, name='rest_kernel', out_shape=[pltpu.HBM((per...  10.7 us
    pallas_call x1, Pallas kernels, finish(): pl.pallas_call(functools.partial(plan_kernel, lead=ga[0].shape[0]), name=...  5.87 us
    pallas_call x1, Pallas kernels, finish(): pl.pallas_call(w_kernel, name='w_kernel', out_shape=cut_tiles(per_cell),...  5.32 us
    pallas_call x1, Pallas kernels, finish(): pl.pallas_call(p_kernel, name='p_kernel', out_shape=[tiles(n) for n in (p...  5.07 us
    pallas_call x1, Pallas kernels, finish(): z3, z4 = pack(fn[0], zl[0], fn[1], zl[1], z)  3.02 us
  transfers between devices with their start and end apart: 12, of which 4 were waited for; matrix products, arithmetic and copies ran while one was open for 0% of the time, Pallas kernels for 22%

profile of v1, /device:TPU:0, one launch (start us, length us, event | category | flops | bytes accessed | tf_op | source)
XLA Modules:
  0.0 122.8 jit_solution(4926365894624079712)
XLA Ops:
  0.7 24.5 %meet_kernel.1 = (f32[8,128,128]{2,1,0:T(8,128)S(1)}, f32[8,128,128]{2,1,0:T(8,128)S(1)}, s32[3,1,64]{2,1,0:T(1,128)S(1)}, s32[3,1,64]{2,1,0:T(1,128)S(1)}, s32[...) custom-call(s32[3,1,64]{2,1,0:T(1,128)} %bitcast.22, ...), custom_call_target="tpu_custom_call" | custom-call | tf_op jit(solution)/shard_map/meet_kernel/pallas_call | solution.py:579
  25.9 96.7 %conditional.1 = (f32[24,128,128]{2,1,0:T(8,128)}, f32[1,1,24,128,128]{4,3,2,1,0:T(8,128)}) conditional(s32[]{:T(128)} %bitcast.12, (s32[3,1,64]{2,1,0:T(1,128)S(1)}, s32[3,1,64]{2,1,0:T(1,128)S(1)}, s32[3,1,64]{2,1,0:T(1,128)S(1)}, s32[3,1,64]{2,1,0:T(1,128)S(1)}, s32[3,1,64]{2,1,0:T(1,128)S(1)}, ...), branch_computations={%region_0.0_spmd, %region_1.0_spmd, %region_2.0_spmd, %region_3.0_... | conditional | flops 15032385536 | bytes 195035856 | solution.py:615
  26.1 3.0 %pack_kernel.9 = (f32[20,128,128]{2,1,0:T(8,128)S(1)}, f32[20,128,128]{2,1,0:T(8,128)S(1)}) custom-call(s32[3,1,64]{2,1,0:T(1,128)S(1)} %get-tuple-element.367.f3, s32[3,1,64]{2,1,0:T(1,128)S(1)} %get-tuple-element.368.z3, s32[3,1,64]{2,1,0:T(1,128)S(1)} %get-tuple-element.369.f4, s32[3,1,64]{2,1,0:T(1,128)S(1)} %get-tuple-element.370.z4, ...), custom_call_target="tpu_custom_call" | custom-call | bytes 6291456 | tf_op jit(solution)/shard_map/cond/branch_3_fun/pack_kernel/pallas_call | solution.py:514
  29.2 0.0 collective-permute-start.37
  29.2 0.5 collective-permute-start.36
  29.7 0.0 collective-permute-start.38
  29.7 5.3 %collective-permute-start.39 = (f32[14,128,128]{2,1,0:T(8,128)}, f32[14,128,128]{2,1,0:T(8,128)S(1)}, u32[]{:S(2)}, u32[]{:S(2)}) collective-permute-start(f32[14,128,128]{2,1,0:T(8,128)} %get-tuple-element.377), channel_id=1, source_target_pairs={{0,15},{1,0},{2,1},{3,2},{4,3},{5,4},{6,5},{7,6},{8,7},{9,8},{10,9... | collective-permute-start | bytes 2752520 | tf_op jit(solution)/shard_map/cond/branch_3_fun/ppermute | solution.py:465
  35.0 0.0 collective-permute-start.44
  35.1 21.2 %collective-permute-done.38.g3 = f32[14,128,128]{2,1,0:T(8,128)S(1)} collective-permute-done((f32[14,128,128]{2,1,0:T(8,128)S(1)}, f32[14,128,128]{2,1,0:T(8,128)S(1)}, u32[]{:S(2)}, u32[]{:S(2)}) %collective-permute-start.38) | collective-permute-done | bytes 917536 | tf_op jit(solution)/shard_map/cond/branch_3_fun/ppermute | solution.py:465
  56.2 1.6 %collective-permute-start.43 = (f32[24,128,128]{2,1,0:T(8,128)}, f32[24,128,128]{2,1,0:T(8,128)S(1)}, u32[]{:S(2)}, u32[]{:S(2)}) collective-permute-start(f32[24,128,128]{2,1,0:T(8,128)} %get-tuple-element.382.z.z0), channel_id=1, source_target_pairs={{0,112},{16,0},{32,16},{48,32},{64,48},{80,64},{96,80},{112,96},{1... | collective-permute-start | bytes 4718600 | tf_op jit(solution)/shard_map/cond/branch_3_fun/ppermute | solution.py:465
  57.9 5.9 %plan_kernel.9 = (s32[32,128]{1,0:T(8,128)S(1)}, bf16[24,128,256]{2,1,0:T(8,128)(2,1)S(1)}, bf16[24,128,256]{2,1,0:T(8,128)(2,1)S(1)}, bf16[24,128,256]{2,1,0:T(8,128)(2,1)S(1)}) custom-call(s32[3,1,64]{2,1,0:T(1,128)S(1)} %get-tuple-element.355.tzg.tasks, s32[3,1,64]{2,1,0:T(1,128)S(1)} %get-tuple-element.352.tfock, ...), custom_call_target="tpu_custom_call" | custom-call | flops 2147483648 | bytes 12582912 | tf_op jit(solution)/shard_map/cond/branch_3_fun/plan_kernel/pallas_call | solution.py:518
  63.8 0.0 collective-permute-start.42
  63.8 0.1 collective-permute-start.45
  64.0 5.3 %w_kernel.9.ws = bf16[24,128,256]{2,1,0:T(8,128)(2,1)S(1)} custom-call(s32[3,1,64]{2,1,0:T(1,128)S(1)} %get-tuple-element.355.tzg.tasks, s32[32,128]{1,0:T(8,128)S(1)} %get-tuple-element.363.plan, bf16[24,128,256]{2,1,0:T(8,128)(2,1)S(1)} %get-tuple-element.365.zs, f32[24,128,128]{2,1,0:T(8,128)} %get-tuple-element.373.g0, ...), custom_call_target="tpu_custom_call" | custom-call | flops 2147483648 | bytes 11010048 | tf_op jit(solution)/shard_map/cond/branch_3_fun/w_kernel/pallas_call | solution.py:528
  69.3 5.1 %p_kernel.9 = (f32[24,128,128]{2,1,0:T(8,128)S(1)}, f32[18,128,128]{2,1,0:T(8,128)S(1)}, f32[18,128,128]{2,1,0:T(8,128)S(1)}, f32[15,128,128]{2,1,0:T(8,128)S(1)}, f32[15,128,128]{2,1,0:T(8,128)S(1)}) custom-call(s32[32,128]{1,0:T(8,128)S(1)} %get-tuple-element.363.plan, bf16[24,128,256]{2,1,0:T(8,128)(2,1)S(1)} %get-tuple-element.378.ft, ...), custom_call_target="tpu_custom_call" | custom-call | flops 4294967296 | bytes 11010048 | tf_op jit(solution)/shard_map/cond/branch_3_fun/p_kernel/pallas_call | solution.py:538
  74.4 0.0 collective-permute-start.40
  74.4 9.7 %collective-permute-done.44.z3 = f32[20,128,128]{2,1,0:T(8,128)S(1)} collective-permute-done((f32[20,128,128]{2,1,0:T(8,128)S(1)}, f32[20,128,128]{2,1,0:T(8,128)S(1)}, u32[]{:S(2)}, u32[]{:S(2)}) %collective-permute-start.44) | collective-permute-done | bytes 1310752 | tf_op jit(solution)/shard_map/cond/branch_3_fun/ppermute | solution.py:465
  84.1 0.7 collective-permute-start.41
  84.8 9.5 %collective-permute-done.45.z4 = f32[20,128,128]{2,1,0:T(8,128)S(1)} collective-permute-done((f32[20,128,128]{2,1,0:T(8,128)S(1)}, f32[20,128,128]{2,1,0:T(8,128)S(1)}, u32[]{:S(2)}, u32[]{:S(2)}) %collective-permute-start.45) | collective-permute-done | bytes 1310752 | tf_op jit(solution)/shard_map/cond/branch_3_fun/ppermute | solution.py:465
  94.3 5.3 %collective-permute-start.47 = (f32[15,128,128]{2,1,0:T(8,128)S(1)}, f32[15,128,128]{2,1,0:T(8,128)S(1)}, u32[]{:S(2)}, u32[]{:S(2)}) collective-permute-start(f32[15,128,128]{2,1,0:T(8,128)S(1)} %get-tuple-element.388), channel_id=1, source_target_pairs={{0,15},{1,0},{2,1},{3,2},{4,3},{5,4},{6,5},{7,6},{8,7},{9,8},{10,9... | collective-permute-start | bytes 2949128 | tf_op jit(solution)/shard_map/cond/branch_3_fun/ppermute | solution.py:465
  99.7 1.1 copy-done.38
  100.8 10.7 %rest_kernel.9 = (f32[24,128,128]{2,1,0:T(8,128)}, f32[24,128,128]{2,1,0:T(8,128)S(1)}) custom-call(s32[3,1,64]{2,1,0:T(1,128)S(1)} %get-tuple-element.352.tfock, s32[3,1,64]{2,1,0:T(1,128)S(1)} %get-tuple-element.353.tfz, s32[3,1,64]{2,1,0:T(1,128)S(1)} %get-tuple-element.354.tzgt, s32[32,128]{1,0:T(8,128)S(1)} %get-tuple-element.363.plan, ...), custom_call_target="tpu_custom_call" | custom-call | flops 6442450944 | bytes 22020096 | tf_op jit(solution)/shard_map/cond/branch_3_fun/rest_kernel/pallas_call | solution.py:549
  111.6 8.6 %collective-permute-done.46.pa = f32[15,128,128]{2,1,0:T(8,128)S(1)} collective-permute-done((f32[15,128,128]{2,1,0:T(8,128)S(1)}, f32[15,128,128]{2,1,0:T(8,128)S(1)}, u32[]{:S(2)}, u32[]{:S(2)}) %collective-permute-start.46) | collective-permute-done | bytes 983072 | tf_op jit(solution)/shard_map/cond/branch_3_fun/ppermute | solution.py:465
  120.2 2.1 %join_kernel.9 = f32[24,128,128]{2,1,0:T(8,128)} custom-call(s32[32,128]{1,0:T(8,128)S(1)} %get-tuple-element.363.plan, f32[24,128,128]{2,1,0:T(8,128)S(1)} %get-tuple-element.386.part, f32[15,128,128]{2,1,0:T(8,128)S(1)} %collective-permute-done.46.pa, f32[15,128,128]{2,1,0:T(8,128)S(1)} %collective-permute-done.47.pb), custom_call_target="tpu_custom_call" | custom-call | bytes 6291456 | tf_op jit(solution)/shard_map/cond/branch_3_fun/join_kernel/pallas_call | solution.py:479
  (30 shorter events, 0.1 us)
Async XLA Ops:
  0.6 25.2 %copy-start.31 = (s32[1,1,3,64]{3,1,2,0:T(1,128)S(1)}, s32[1,1,3,64]{3,1,2,0:T(1,128)}, u32[]{:S(2)}) copy-start(s32[1,1,3,64]{3,1,2,0:T(1,128)} %param.21) | copy-start | bytes 2308
  0.6 25.2 %copy-start.30 = (s32[1,1,3,64]{3,1,2,0:T(1,128)S(1)}, s32[1,1,3,64]{3,1,2,0:T(1,128)}, u32[]{:S(2)}) copy-start(s32[1,1,3,64]{3,1,2,0:T(1,128)} %param.20) | copy-start | bytes 2308
  0.7 25.2 %copy-start.29 = (s32[1,1,3,64]{3,1,2,0:T(1,128)S(1)}, s32[1,1,3,64]{3,1,2,0:T(1,128)}, u32[]{:S(2)}) copy-start(s32[1,1,3,64]{3,1,2,0:T(1,128)} %param.19) | copy-start | bytes 2308
  0.7 25.2 %copy-start.28 = (s32[1,1,3,64]{3,1,2,0:T(1,128)S(1)}, s32[1,1,3,64]{3,1,2,0:T(1,128)}, u32[]{:S(2)}) copy-start(s32[1,1,3,64]{3,1,2,0:T(1,128)} %param.18) | copy-start | bytes 2308
  0.7 25.2 %copy-start.27 = (s32[1,1,3,64]{3,1,2,0:T(1,128)S(1)}, s32[1,1,3,64]{3,1,2,0:T(1,128)}, u32[]{:S(2)}) copy-start(s32[1,1,3,64]{3,1,2,0:T(1,128)} %param.17) | copy-start | bytes 2308
  0.7 25.2 %copy-start.32 = (f32[1,1,24,128,128]{4,3,2,1,0:T(8,128)S(1)}, f32[1,1,24,128,128]{4,3,2,1,0:T(8,128)}, u32[]{:S(2)}) copy-start(f32[1,1,24,128,128]{4,3,2,1,0:T(8,128)} %param.15) | copy-start | bytes 4718596
  26.1 3.6 %copy-start.43 = (f32[14,128,128]{2,1,0:T(8,128)S(1)}, f32[14,128,128]{2,1,0:T(8,128)}, u32[]{:S(2)}) copy-start(f32[14,128,128]{2,1,0:T(8,128)} %get-tuple-element.375) | copy-start | bytes 2752516 | tf_op jit(solution)/shard_map/cond
  29.2 34.6 %collective-permute-start.37 = (f32[24,128,128]{2,1,0:T(8,128)}, f32[24,128,128]{2,1,0:T(8,128)S(1)}, u32[]{:S(2)}, u32[]{:S(2)}) collective-permute-start(f32[24,128,128]{2,1,0:T(8,128)} %get-tuple-element.373.g0), channel_id=1, source_target_pairs={{0,112},{16,0},{32,16},{48,32},{64,48},{80,64},{96,80},{112,96},{1... | collective-permute-start | bytes 4718600 | tf_op jit(solution)/shard_map/cond/branch_3_fun/ppermute | solution.py:465
  29.2 34.7 %collective-permute-start.36 = (f32[24,128,128]{2,1,0:T(8,128)}, f32[24,128,128]{2,1,0:T(8,128)S(1)}, u32[]{:S(2)}, u32[]{:S(2)}) collective-permute-start(f32[24,128,128]{2,1,0:T(8,128)} %get-tuple-element.373.g0), channel_id=1, source_target_pairs={{0,16},{16,32},{32,48},{48,64},{64,80},{80,96},{96,112},{112,0},{1... | collective-permute-start | bytes 4718600 | tf_op jit(solution)/shard_map/cond/branch_3_fun/ppermute | solution.py:465
  29.7 26.5 %collective-permute-start.38 = (f32[14,128,128]{2,1,0:T(8,128)S(1)}, f32[14,128,128]{2,1,0:T(8,128)S(1)}, u32[]{:S(2)}, u32[]{:S(2)}) collective-permute-start(f32[14,128,128]{2,1,0:T(8,128)S(1)} %copy-done.43), channel_id=1, source_target_pairs={{0,1},{1,2},{2,3},{3,4},{4,5},{5,6},{6,7},{7,8},{8,9},{9,10},{10,1... | collective-permute-start | bytes 2752520 | tf_op jit(solution)/shard_map/cond/branch_3_fun/ppermute | solution.py:465
  29.7 34.0 %collective-permute-start.39 = (f32[14,128,128]{2,1,0:T(8,128)}, f32[14,128,128]{2,1,0:T(8,128)S(1)}, u32[]{:S(2)}, u32[]{:S(2)}) collective-permute-start(f32[14,128,128]{2,1,0:T(8,128)} %get-tuple-element.377), channel_id=1, source_target_pairs={{0,15},{1,0},{2,1},{3,2},{4,3},{5,4},{6,5},{7,6},{8,7},{9,8},{10,9... | collective-permute-start | bytes 2752520 | tf_op jit(solution)/shard_map/cond/branch_3_fun/ppermute | solution.py:465
  35.0 49.1 %collective-permute-start.44 = (f32[20,128,128]{2,1,0:T(8,128)S(1)}, f32[20,128,128]{2,1,0:T(8,128)S(1)}, u32[]{:S(2)}, u32[]{:S(2)}) collective-permute-start(f32[20,128,128]{2,1,0:T(8,128)S(1)} %get-tuple-element.383), channel_id=1, source_target_pairs={{0,1},{1,2},{2,3},{3,4},{4,5},{5,6},{6,7},{7,8},{8,9},{9,10},{10,1... | collective-permute-start | bytes 3932168 | tf_op jit(solution)/shard_map/cond/branch_3_fun/ppermute | solution.py:465
  56.2 38.1 %collective-permute-start.43 = (f32[24,128,128]{2,1,0:T(8,128)}, f32[24,128,128]{2,1,0:T(8,128)S(1)}, u32[]{:S(2)}, u32[]{:S(2)}) collective-permute-start(f32[24,128,128]{2,1,0:T(8,128)} %get-tuple-element.382.z.z0), channel_id=1, source_target_pairs={{0,112},{16,0},{32,16},{48,32},{64,48},{80,64},{96,80},{112,96},{1... | collective-permute-start | bytes 4718600 | tf_op jit(solution)/shard_map/cond/branch_3_fun/ppermute | solution.py:465
  63.8 35.9 %collective-permute-start.42 = (f32[24,128,128]{2,1,0:T(8,128)}, f32[24,128,128]{2,1,0:T(8,128)S(1)}, u32[]{:S(2)}, u32[]{:S(2)}) collective-permute-start(f32[24,128,128]{2,1,0:T(8,128)} %get-tuple-element.382.z.z0), channel_id=1, source_target_pairs={{0,16},{16,32},{32,48},{48,64},{64,80},{80,96},{96,112},{112,0},{1... | collective-permute-start | bytes 4718600 | tf_op jit(solution)/shard_map/cond/branch_3_fun/ppermute | solution.py:465
  63.8 5.5 %copy-start.3 = (f32[24,128,128]{2,1,0:T(8,128)}, f32[24,128,128]{2,1,0:T(8,128)S(1)}, u32[]{:S(2)}) copy-start(f32[24,128,128]{2,1,0:T(8,128)S(1)} %collective-permute-done.37.g2) | copy-start | bytes 4718596 | tf_op jit(solution)/shard_map/cond
  63.8 30.5 %collective-permute-start.45 = (f32[20,128,128]{2,1,0:T(8,128)S(1)}, f32[20,128,128]{2,1,0:T(8,128)S(1)}, u32[]{:S(2)}, u32[]{:S(2)}) collective-permute-start(f32[20,128,128]{2,1,0:T(8,128)S(1)} %get-tuple-element.384), channel_id=1, source_target_pairs={{0,15},{1,0},{2,1},{3,2},{4,3},{5,4},{6,5},{7,6},{8,7},{9,8},{10,9... | collective-permute-start | bytes 3932168 | tf_op jit(solution)/shard_map/cond/branch_3_fun/ppermute | solution.py:465
  64.0 5.3 %copy-start.9 = (f32[24,128,128]{2,1,0:T(8,128)}, f32[24,128,128]{2,1,0:T(8,128)S(1)}, u32[]{:S(2)}) copy-start(f32[24,128,128]{2,1,0:T(8,128)S(1)} %collective-permute-done.36.g1) | copy-start | bytes 4718596 | tf_op jit(solution)/shard_map/cond
  74.4 25.3 %collective-permute-start.40 = (f32[18,128,128]{2,1,0:T(8,128)S(1)}, f32[18,128,128]{2,1,0:T(8,128)S(1)}, u32[]{:S(2)}, u32[]{:S(2)}) collective-permute-start(f32[18,128,128]{2,1,0:T(8,128)S(1)} %get-tuple-element.380), channel_id=1, source_target_pairs={{0,16},{16,32},{32,48},{48,64},{64,80},{80,96},{96,112},{112,0},{1... | collective-permute-start | bytes 3538952 | tf_op jit(solution)/shard_map/cond/branch_3_fun/ppermute | solution.py:465
  84.1 15.5 %collective-permute-start.41 = (f32[18,128,128]{2,1,0:T(8,128)S(1)}, f32[18,128,128]{2,1,0:T(8,128)S(1)}, u32[]{:S(2)}, u32[]{:S(2)}) collective-permute-start(f32[18,128,128]{2,1,0:T(8,128)S(1)} %get-tuple-element.381), channel_id=1, source_target_pairs={{0,112},{16,0},{32,16},{48,32},{64,48},{80,64},{96,80},{112,96},{1... | collective-permute-start | bytes 3538952 | tf_op jit(solution)/shard_map/cond/branch_3_fun/ppermute | solution.py:465
  94.3 25.9 %collective-permute-start.46 = (f32[15,128,128]{2,1,0:T(8,128)S(1)}, f32[15,128,128]{2,1,0:T(8,128)S(1)}, u32[]{:S(2)}, u32[]{:S(2)}) collective-permute-start(f32[15,128,128]{2,1,0:T(8,128)S(1)} %get-tuple-element.387), channel_id=1, source_target_pairs={{0,1},{1,2},{2,3},{3,4},{4,5},{5,6},{6,7},{7,8},{8,9},{9,10},{10,1... | collective-permute-start | bytes 2949128 | tf_op jit(solution)/shard_map/cond/branch_3_fun/ppermute | solution.py:465
  94.3 5.4 %copy-start.35 = (f32[24,128,128]{2,1,0:T(8,128)}, f32[24,128,128]{2,1,0:T(8,128)S(1)}, u32[]{:S(2)}) copy-start(f32[24,128,128]{2,1,0:T(8,128)S(1)} %collective-permute-done.43.z2) | copy-start | bytes 4718596 | tf_op jit(solution)/shard_map/cond
  94.3 25.9 %collective-permute-start.47 = (f32[15,128,128]{2,1,0:T(8,128)S(1)}, f32[15,128,128]{2,1,0:T(8,128)S(1)}, u32[]{:S(2)}, u32[]{:S(2)}) collective-permute-start(f32[15,128,128]{2,1,0:T(8,128)S(1)} %get-tuple-element.388), channel_id=1, source_target_pairs={{0,15},{1,0},{2,1},{3,2},{4,3},{5,4},{6,5},{7,6},{8,7},{9,8},{10,9... | collective-permute-start | bytes 2949128 | tf_op jit(solution)/shard_map/cond/branch_3_fun/ppermute | solution.py:465
  99.7 1.1 copy-start.38

commit v2 on v1

--- a/solution.py
+++ b/solution.py
@@ -124,8 +124,8 @@
         below = (lax.broadcasted_iota(I32, square, 1) < lax.broadcasted_iota(I32, square, 0)).astype(F32)
         return jnp.dot(below, jnp.broadcast_to(found, self.number.shape).astype(F32), preferred_element_type=F32)
 
-    def packed_rows(self, found):
-        spread = jnp.broadcast_to(self.lane, self.number.shape).astype(F32)
+    def packed_rows(self, found, first=0):
+        spread = jnp.broadcast_to(self.lane - first, self.number.shape).astype(F32)
         here = jnp.logical_and(self.ranked(found) == spread, jnp.broadcast_to(found, self.number.shape) == 1)
         order = jnp.sum(jnp.where(here, self.number, 0), axis=0, keepdims=True)
         return jnp.where(self.lane == TILE - 1, jnp.sum(found), order)
@@ -134,13 +134,13 @@
         rank = self.ranked(found)[:, : self.length].astype(I32)
         return jnp.sum(jnp.where(self.hits(key), rank, 0), axis=0, keepdims=True)
 
-    def places(self, tasks, lists, first=0):
+    def places(self, tasks, lists, first, starts):
         place = tasks[2]
         for k in (3, 4):
             key = tasks[2] - k * self.per_cell
             here = jnp.logical_and(key >= first, key < self.per_cell)
             rank = self.rank_of(key, self.of_cell(lists, k, first))
-            place = jnp.where(here, k * self.per_cell + first + rank, place)
+            place = jnp.where(here, starts[k] + rank, place)
         return place
 
 
@@ -151,11 +151,10 @@
     return result
 
 
-def meet_kernel(tzg, tfock, tfz, tzgt, ttrans, g, *refs, rooms, g_rooms, lead, cuts):
-    packs = 2 * len(g_rooms)
-    ga, tn, fn, zl, gp = refs[:2], refs[2:6], refs[6:8], refs[8:10], refs[10 : 10 + packs]
-    (level, gl, gt, msg, line, lines, pick, picked, gv, packed, bulk_s, bulk_r, list_s, list_r) = refs[10 + packs : 24 + packs]
-    line_s, line_r, lines_s, lines_r, own, put = refs[24 + packs :]
+def meet_kernel(tzg, tfock, tfz, tzgt, ttrans, g, z, *refs, rooms, lead, cuts):
+    ga, tn, gp = refs[:2], refs[2:6], refs[6:8]
+    (level, pick, gl, gt, fl, zl, msg, line, lines, picked, source, packed, bulk_s, bulk_r, list_s, list_r) = refs[8:24]
+    line_s, line_r, lines_s, lines_r, own, put = refs[24:]
     ny, nx = line.shape[0], lines.shape[0]
     per_cell = g.shape[0]
     ix, iy = lax.axis_index("gx"), lax.axis_index("gy")
@@ -164,8 +163,13 @@
         pl.semaphore_signal(barrier, inc=1, device_id=(lax.rem(ix + j, nx), iy), device_id_type=MESH)
     for j in range(1, ny):
         pl.semaphore_signal(barrier, inc=1, device_id=(ix, lax.rem(iy + j, ny)), device_id_type=MESH)
-    load = pltpu.make_async_copy(g.at[pl.ds(lead, per_cell - lead)], gv, own.at[3])
-    load.start()
+    rest_g = per_cell - lead
+    loads = [
+        pltpu.make_async_copy(g.at[pl.ds(lead, rest_g)], source.at[pl.ds(0, rest_g)], own.at[3]),
+        pltpu.make_async_copy(z, source.at[pl.ds(rest_g, per_cell)], own.at[4]),
+    ]
+    for c in loads:
+        c.start()
     others = []
     for axis, by in STEPS:
         others.append((lax.rem(ix + by + nx, nx), iy) if axis == "gx" else (ix, lax.rem(iy + by + ny, ny)))
@@ -184,7 +188,7 @@
     lists = []
     for i in range(2):
         lists += [(tzg, gl.at[i], others[2 + i]), (tzgt, gt.at[i], others[2 + i])]
-        lists += [(tfock, fn[i], others[2 + i]), (tfz, zl[i], others[2 + i])]
+        lists += [(tfock, fl.at[i], others[2 + i]), (tfz, zl.at[i], others[2 + i])]
     lists += [(ttrans, tn[k], others[k]) for k in range(4)]
     small = []
     for i, (src, dst, to) in enumerate(lists):
@@ -197,10 +201,10 @@
         return functools.reduce(jnp.maximum, [jnp.sum(v) for v in found])
 
     needs = (
-        most([tables.of_cell((tzg, tzgt), k, lead) for k in (3, 4)]),
-        most([tables.of_cell((tfock, tfz), k) for k in (3, 4)]),
+        most([tables.of_cell((tzg, tzgt), k, lead) + tables.of_cell((tfock, tfz), k) for k in (3, 4)]),
         most([tables.named((tables.outs(ttrans, k),)) for k in (1, 2)]),
         most([tables.named((tables.outs(ttrans, k),)) for k in (3, 4)]),
+        0,
     )
     msg[...] = by_quarter(tables.lane, needs)
     keep = pltpu.make_async_copy(msg, line.at[pl.ds(0, 1)], own.at[0])
@@ -227,24 +231,28 @@
     for c in small:
         c.wait()
 
+    pick[...] = jnp.zeros_like(pick)
     for side in range(2):
-        order = tables.packed_rows(tables.of_cell((gl.at[side], gt.at[side]), 3 + side, lead))
-        pick[side : side + 1, :] = jnp.maximum(order - lead, 0)
+        g_named = tables.of_cell((gl.at[side], gt.at[side]), 3 + side, lead)
+        z_named = tables.of_cell((fl.at[side], zl.at[side]), 3 + side)
+        count = jnp.sum(g_named)
+        order = jnp.where(tables.lane < count, tables.packed_rows(g_named) - lead, tables.packed_rows(z_named, count) + rest_g)
+        pick[side : side + 1, :] = jnp.clip(order, 0, rest_g + per_cell - 1)
     copy = pltpu.make_async_copy(pick, picked, own.at[2])
     copy.start()
     copy.wait()
-    load.wait()
+    for c in loads:
+        c.wait()
     puts = []
     for side in range(2):
 
         def take(s, _, side=side):
-            packed[side, s] = gv[picked[side, s]]
+            packed[side, s] = source[picked[side, s]]
             return 0
 
-        lax.fori_loop(0, per_cell - lead, take, 0)
-        for i, room in enumerate(g_rooms):
-            puts.append(pltpu.make_async_copy(packed.at[side, pl.ds(0, room)], gp[2 * i + side], put.at[2 * i + side]))
-            puts[-1].start()
+        lax.fori_loop(0, rest_g, take, 0)
+        puts.append(pltpu.make_async_copy(packed.at[side], gp[side], put.at[side]))
+        puts[-1].start()
     keep.wait()
     for c in second:
         c.wait()
@@ -261,19 +269,13 @@
         c.wait()
 
 
-def pack_kernel(f3, z3, f4, z4, z, out3, out4, pick, packed, picked, own, put):
+def pack_kernel(pick, z, out3, out4, packed, put, *, first):
     per_cell, room = z.shape[0], out3.shape[0]
-    tables = Tables(per_cell, f3.shape[2])
-    for side, lists in enumerate(((f3, z3), (f4, z4))):
-        pick[side : side + 1, :] = tables.packed_rows(tables.of_cell(lists, 3 + side))
-    copy = pltpu.make_async_copy(pick, picked, own)
-    copy.start()
-    copy.wait()
     puts = []
     for side, out in enumerate((out3, out4)):
 
         def take(s, _, side=side):
-            packed[side, s] = z[picked[side, s]]
+            packed[side, s] = z[jnp.clip(pick[side, first + s] - first, 0, per_cell - 1)]
             return 0
 
         lax.fori_loop(0, room, take, 0)
@@ -281,6 +283,10 @@
         puts[-1].start()
     for c in puts:
         c.wait()
+
+
+def run_start(per_cell, lead, k):
+    return 3 * per_cell + (k - 3) * (2 * per_cell - lead)
 
 
 def plan_kernel(tzg, tfock, tfz, tzgt, t0, t1, t2, t3, t4, f, z, plan, fs, ft, zs, table, cut, put, *, lead):
@@ -300,13 +306,15 @@
     tables = Tables(per_cell, length)
     lane = tables.lane
     plan[...] = jnp.zeros_like(plan)
-    for at, tasks, lists, first in (
-        (FOCK_ROW, tfock, (tfock, tfz), 0),
-        (FZ_ROW, tfz, (tfock, tfz), 0),
-        (ZG_ROW, tzg, (tzg, tzgt), lead),
-        (ZGT_ROW, tzgt, (tzg, tzgt), lead),
+    g_starts = {k: k * per_cell + lead for k in (3, 4)}
+    z_starts = {k: run_start(per_cell, lead, k) + jnp.sum(tables.of_cell((tzg, tzgt), k, lead)) for k in (3, 4)}
+    for at, tasks, lists, first, starts in (
+        (FOCK_ROW, tfock, (tfock, tfz), 0, z_starts),
+        (FZ_ROW, tfz, (tfock, tfz), 0, z_starts),
+        (ZG_ROW, tzg, (tzg, tzgt), lead, g_starts),
+        (ZGT_ROW, tzgt, (tzg, tzgt), lead, g_starts),
     ):
-        plan[at : at + 1, pl.ds(0, length)] = tables.places(tasks, lists, first)
+        plan[at : at + 1, pl.ds(0, length)] = tables.places(tasks, lists, first, starts)
     for k in range(1, 5):
         plan[MAP_ROW + k - 1 : MAP_ROW + k, :] = tables.packed_rows(tables.named((tables.outs(t0, k),)))
     square = (length, length)
@@ -391,7 +399,11 @@
 
 def rest_kernel(tfock, tfz, tzgt, plan, fs, ws, p0, p1, p2, z0, z1, z2, z3, z4, g0, g1, g2, a3, g3, a4, g4, fock, factor, zgrown, ggrown, us, total, zsem, gsem, osem):
     per_cell, lead = p0.shape[0], a3.shape[0]
-    zcopies = fetch([(src, k * per_cell) for k, src in enumerate((z0, z1, z2, z3, z4))], zgrown, zsem)
+    places = [(src, k * per_cell) for k, src in enumerate((z0, z1, z2))]
+    for k, first, then in ((3, g3, z3), (4, g4, z4)):
+        start = run_start(per_cell, lead, k)
+        places += [(first, start), (then, start + first.shape[0])]
+    zcopies = fetch(places, zgrown, zsem)
     gcopies = fetch(g_places(per_cell, lead, g0, g1, g2, a3, g3, a4, g4), ggrown, gsem)
     clear(total.at[0], 0, per_cell)
     clear(total.at[1], 0, per_cell)
@@ -488,30 +500,26 @@
     )(plan, part, pa, pb)
 
 
-def finish(z_room, x_room, y_room, gp3, gp4, z, f, g, tzg, tfock, tfz, tzgt, ttrans, tn, fn, zl, ga):
+def finish(run_room, x_room, y_room, gp, z, f, g, tzg, tfock, tfz, tzgt, ttrans, tn, pick, ga):
     per_cell = z.shape[0]
     cap = tzg.shape[2]
     grown = pltpu.VMEM((5 * per_cell, TILE, TILE), F32)
     cut = pltpu.VMEM((per_cell, TILE, 2 * TILE), jnp.bfloat16)
     params = pltpu.CompilerParams(vmem_limit_bytes=40 * 2**20)
-    gy = (shifted(gp3, "gy", 1), shifted(gp4, "gy", -1))
+    gy = (shifted(gp[0], "gy", 1), shifted(gp[1], "gy", -1))
+    first = gp[0].shape[0]
+    z_room = run_room - first
     pack = pl.pallas_call(
-        pack_kernel,
+        functools.partial(pack_kernel, first=first),
         name="pack_kernel",
         out_shape=[tiles(z_room)] * 2,
-        in_specs=[VMEM] * 5,
+        in_specs=[SMEM, VMEM],
         out_specs=[ANY] * 2,
-        scratch_shapes=[
-            pltpu.VMEM((8, TILE), I32),
-            pltpu.VMEM((2, z_room, TILE, TILE), F32),
-            pltpu.SMEM((8, TILE), I32),
-            DMA,
-            DMA((2,)),
-        ],
+        scratch_shapes=[pltpu.VMEM((2, z_room, TILE, TILE), F32), DMA((2,))],
         compiler_params=pltpu.CompilerParams(vmem_limit_bytes=16 * 2**20),
         cost_estimate=cost(0, 4 * per_cell),
     )
-    z3, z4 = pack(fn[0], zl[0], fn[1], zl[1], z)
+    z3, z4 = pack(pick, z)
     g_late, z_late, z3, z4 = lax.optimization_barrier((g, z, z3, z4))
     gn = (shifted(g_late, "gx", 1), shifted(g_late, "gx", -1), ga[0], gy[0], ga[1], gy[1])
     zn = (shifted(z_late, "gx", 1), shifted(z_late, "gx", -1), shifted(z3, "gy", 1), shifted(z4, "gy", -1))
@@ -552,7 +560,15 @@
         out_shape=[pltpu.HBM((per_cell, TILE, TILE), F32), tiles(per_cell)],
         in_specs=[SMEM] * 4 + [VMEM] * 5 + [ANY] * 12,
         out_specs=[HBM, ANY],
-        scratch_shapes=[grown, grown, cut, pltpu.VMEM((3, per_cell + 1, TILE, TILE), F32), DMA((5,)), DMA((7,)), DMA((2,))],
+        scratch_shapes=[
+            pltpu.VMEM((run_start(per_cell, ga[0].shape[0], 5), TILE, TILE), F32),
+            grown,
+            cut,
+            pltpu.VMEM((3, per_cell + 1, TILE, TILE), F32),
+            DMA((7,)),
+            DMA((7,)),
+            DMA((2,)),
+        ],
         compiler_params=params,
         cost_estimate=cost(3 * cap, 14 * per_cell),
     )(tfock, tfz, tzgt, plan, fs, ws, p[0], pn[0], pn[1], z, *zn, g, *gn)
@@ -560,9 +576,9 @@
 
 
 def rooms_of(per_cell, lead):
-    levels = ((13, 18, 18, 12), (14, 18, 18, 13), (13, 19, 18, 14), (14, 20, 18, 15), (16, 22, 18, 17))
+    levels = ((29, 18, 12), (29, 18, 14), (30, 18, 13), (31, 18, 15), (34, 18, 17))
     scaled = [tuple(per_cell * room // 24 for room in level) for level in levels]
-    return scaled + [(per_cell - lead,) + (per_cell,) * 3]
+    return scaled + [(2 * per_cell - lead, per_cell, per_cell)]
 
 
 def body(z_factor, fock, cotangent, tasks_zg, tasks_fock, tasks_fz, tasks_zgt, tasks_trans):
@@ -574,23 +590,22 @@
     a_list = jax.ShapeDtypeStruct(tzg.shape, I32)
     lead = per_cell // 3
     rooms = rooms_of(per_cell, lead)
-    g_rooms = sorted({room[0] for room in rooms})
-    packs = 2 * len(g_rooms)
     met = pl.pallas_call(
-        functools.partial(meet_kernel, rooms=rooms, g_rooms=g_rooms, lead=lead, cuts=lead // 4),
+        functools.partial(meet_kernel, rooms=rooms, lead=lead, cuts=lead // 4),
         name="meet_kernel",
-        out_shape=[tiles(lead)] * 2 + [a_list] * 8 + [tiles(room) for room in g_rooms for _ in range(2)] + [jax.ShapeDtypeStruct((1, 1), I32)],
-        in_specs=[VMEM] * 5 + [ANY],
-        out_specs=[ANY] * 2 + [VMEM] * 8 + [ANY] * packs + [SMEM],
-        scratch_shapes=[
-            pltpu.VMEM((2,) + tzg.shape, I32),
-            pltpu.VMEM((2,) + tzg.shape, I32),
+        out_shape=[tiles(lead)] * 2
+        + [a_list] * 4
+        + [tiles(per_cell - lead)] * 2
+        + [jax.ShapeDtypeStruct((1, 1), I32), jax.ShapeDtypeStruct((8, TILE), I32)],
+        in_specs=[VMEM] * 5 + [ANY] * 2,
+        out_specs=[ANY] * 2 + [VMEM] * 4 + [ANY] * 2 + [SMEM, VMEM],
+        scratch_shapes=[pltpu.VMEM((2,) + tzg.shape, I32)] * 4
+        + [
             pltpu.VMEM((1, TILE), I32),
             pltpu.VMEM((ny, TILE), I32),
             pltpu.VMEM((nx, ny, TILE), I32),
-            pltpu.VMEM((8, TILE), I32),
             pltpu.SMEM((8, TILE), I32),
-            pltpu.VMEM((per_cell - lead, TILE, TILE), F32),
+            pltpu.VMEM((2 * per_cell - lead, TILE, TILE), F32),
             pltpu.VMEM((2, per_cell - lead, TILE, TILE), F32),
             DMA((4,)),
             DMA((4,)),
@@ -600,19 +615,14 @@
             DMA((ny,)),
             DMA((nx,)),
             DMA((nx,)),
-            DMA((4,)),
-            DMA((packs,)),
+            DMA((5,)),
+            DMA((2,)),
         ],
         compiler_params=pltpu.CompilerParams(collective_id=0, has_side_effects=True),
-    )(tzg, tfock, tfz, tzgt, ttrans, g)
-    ga, tn, fn, zl, gp, level = met[:2], met[2:6], met[6:8], met[8:10], met[10 : 10 + packs], met[-1]
-
-    def branch(g_room, z_room, x_room, y_room):
-        at = 2 * g_rooms.index(g_room)
-        return lambda gp, *rest: finish(z_room, x_room, y_room, gp[at], gp[at + 1], *rest)
-
-    operands = (gp, z, f, g, tzg, tfock, tfz, tzgt, ttrans, tn, fn, zl, ga)
-    fock_grad, factor_grad = lax.switch(level[0, 0], [branch(*room) for room in rooms], *operands)
+    )(tzg, tfock, tfz, tzgt, ttrans, g, z)
+    ga, tn, gp, level, pick = met[:2], met[2:6], met[6:8], met[8], met[9]
+    operands = (gp, z, f, g, tzg, tfock, tfz, tzgt, ttrans, tn, pick, ga)
+    fock_grad, factor_grad = lax.switch(level[0, 0], [functools.partial(finish, *room) for room in rooms], *operands)
     return fock_grad[None, None], factor_grad[None, None]
 
 

time: 123 us -> 126 us (1.024)
  the two profiles are of different devices: /device:TPU:0 before, /device:TPU:24 now
where the time goes in v2:
time: 126 us
  waiting for transfers between devices  56 us (44%)
  Pallas kernels  46.7 us (37%)
  starting transfers between devices  18.5 us (15%)
  local copies, waits for them, and re-layouts  2.58 us (2%)
  between operations  1.58 us (1%)
    ppermute x12, waiting for transfers between devices, shifted(): return lax.ppermute(array, axis, [(i, (i + by) % n) for i in range(n)])  56 us
    pallas_call x1, Pallas kernels, body(): pl.pallas_call(functools.partial(meet_kernel, rooms=rooms, lead=lead, cut...  22.4 us
    ppermute x12, starting transfers between devices, shifted(): return lax.ppermute(array, axis, [(i, (i + by) % n) for i in range(n)])  18.5 us
    pallas_call x1, Pallas kernels, finish(): pl.pallas_call(rest_kernel, name='rest_kernel', out_shape=[pltpu.HBM((per...  6.11 us
    pallas_call x1, Pallas kernels, finish(): pl.pallas_call(functools.partial(plan_kernel, lead=ga[0].shape[0]), name=...  5.92 us
    pallas_call x1, Pallas kernels, finish(): pl.pallas_call(w_kernel, name='w_kernel', out_shape=cut_tiles(per_cell),...  4 us
    pallas_call x1, Pallas kernels, finish(): pl.pallas_call(p_kernel, name='p_kernel', out_shape=[tiles(n) for n in (p...  3.9 us
    cond x12, local copies, waits for them, and re-layouts  2.56 us
  transfers between devices with their start and end apart: 12, of which 3 were waited for; matrix products, arithmetic and copies ran while one was open for 0% of the time, Pallas kernels for 16%

profile of v2, /device:TPU:24, one launch (start us, length us, event | category | flops | bytes accessed | tf_op | source)
XLA Modules:
  0.0 126.2 jit_solution(16450569541018852074)
XLA Ops:
  0.7 22.4 %meet_kernel.1 = (f32[8,128,128]{2,1,0:T(8,128)S(1)}, f32[8,128,128]{2,1,0:T(8,128)S(1)}, s32[3,1,64]{2,1,0:T(1,128)S(1)}, s32[3,1,64]{2,1,0:T(1,128)S(1)}, s32[...) custom-call(s32[3,1,64]{2,1,0:T(1,128)} %bitcast.22, ...), custom_call_target="tpu_custom_call" | custom-call | tf_op jit(solution)/shard_map/meet_kernel/pallas_call | solution.py:593
  23.8 102.2 %conditional.1 = (f32[24,128,128]{2,1,0:T(8,128)}, f32[1,1,24,128,128]{4,3,2,1,0:T(8,128)}) conditional(s32[]{:T(128)} %bitcast.13, (s32[3,1,64]{2,1,0:T(1,128)S(1)}, s32[3,1,64]{2,1,0:T(1,128)S(1)}, s32[3,1,64]{2,1,0:T(1,128)S(1)}, s32[3,1,64]{2,1,0:T(1,128)S(1)}, s32[3,1,64]{2,1,0:T(1,128)S(1)}, ...), branch_computations={%region_0.0_spmd, %region_1.0_spmd, %region_2.0_spmd, %region_3.0_... | conditional | flops 15032385536 | bytes 195035856 | solution.py:625
  24.0 2.4 %pack_kernel.8 = (f32[14,128,128]{2,1,0:T(8,128)S(1)}, f32[14,128,128]{2,1,0:T(8,128)S(1)}) custom-call(s32[8,128]{1,0:T(8,128)S(1)} %get-tuple-element.288.pick, f32[24,128,128]{2,1,0:T(8,128)} %get-tuple-element.300.z.z0), custom_call_target="tpu_custom_call" | custom-call | bytes 6291456 | tf_op jit(solution)/shard_map/cond/branch_2_fun/pack_kernel/pallas_call | solution.py:522
  26.4 0.0 collective-permute-start.25
  26.4 0.5 collective-permute-start.24
  26.9 0.5 collective-permute-start.26
  27.4 4.9 %collective-permute-start.27 = (f32[16,128,128]{2,1,0:T(8,128)}, f32[16,128,128]{2,1,0:T(8,128)S(1)}, u32[]{:S(2)}, u32[]{:S(2)}) collective-permute-start(f32[16,128,128]{2,1,0:T(8,128)} %get-tuple-element.295), channel_id=1, source_target_pairs={{0,15},{1,0},{2,1},{3,2},{4,3},{5,4},{6,5},{7,6},{8,7},{9,8},{10,9... | collective-permute-start | bytes 3145736 | tf_op jit(solution)/shard_map/cond/branch_2_fun/ppermute | solution.py:477
  32.3 23.2 %collective-permute-done.26.g3 = f32[16,128,128]{2,1,0:T(8,128)S(1)} collective-permute-done((f32[16,128,128]{2,1,0:T(8,128)S(1)}, f32[16,128,128]{2,1,0:T(8,128)S(1)}, u32[]{:S(2)}, u32[]{:S(2)}) %collective-permute-start.26) | collective-permute-done | bytes 1048608 | tf_op jit(solution)/shard_map/cond/branch_2_fun/ppermute | solution.py:477
  55.5 1.1 collective-permute-start.31
  56.5 5.9 %plan_kernel.8 = (s32[32,128]{1,0:T(8,128)S(1)}, bf16[24,128,256]{2,1,0:T(8,128)(2,1)S(1)}, bf16[24,128,256]{2,1,0:T(8,128)(2,1)S(1)}, bf16[24,128,256]{2,1,0:T(8,128)(2,1)S(1)}) custom-call(s32[3,1,64]{2,1,0:T(1,128)S(1)} %get-tuple-element.276.tzg.tasks, s32[3,1,64]{2,1,0:T(1,128)S(1)} %get-tuple-element.273.tfock, ...), custom_call_target="tpu_custom_call" | custom-call | flops 2147483648 | bytes 12582912 | tf_op jit(solution)/shard_map/cond/branch_2_fun/plan_kernel/pallas_call | solution.py:526
  62.4 0.7 collective-permute-start.30
  63.2 4.0 %w_kernel.8.ws = bf16[24,128,256]{2,1,0:T(8,128)(2,1)S(1)} custom-call(s32[3,1,64]{2,1,0:T(1,128)S(1)} %get-tuple-element.276.tzg.tasks, s32[32,128]{1,0:T(8,128)S(1)} %get-tuple-element.284.plan, bf16[24,128,256]{2,1,0:T(8,128)(2,1)S(1)} %get-tuple-element.286.zs, f32[24,128,128]{2,1,0:T(8,128)} %get-tuple-element.291.g0, ...), custom_call_target="tpu_custom_call" | custom-call | flops 2147483648 | bytes 11010048 | tf_op jit(solution)/shard_map/cond/branch_2_fun/w_kernel/pallas_call | solution.py:536
  67.2 3.9 %p_kernel.8 = (f32[24,128,128]{2,1,0:T(8,128)S(1)}, f32[18,128,128]{2,1,0:T(8,128)S(1)}, f32[18,128,128]{2,1,0:T(8,128)S(1)}, f32[13,128,128]{2,1,0:T(8,128)S(1)}, f32[13,128,128]{2,1,0:T(8,128)S(1)}) custom-call(s32[32,128]{1,0:T(8,128)S(1)} %get-tuple-element.284.plan, bf16[24,128,256]{2,1,0:T(8,128)(2,1)S(1)} %get-tuple-element.296.ft, ...), custom_call_target="tpu_custom_call" | custom-call | flops 4294967296 | bytes 11010048 | tf_op jit(solution)/shard_map/cond/branch_2_fun/p_kernel/pallas_call | solution.py:546
  71.1 0.0 copy-start.22
  71.1 1.1 copy-done.22
  72.2 4.0 %collective-permute-start.28 = (f32[18,128,128]{2,1,0:T(8,128)S(1)}, f32[18,128,128]{2,1,0:T(8,128)S(1)}, u32[]{:S(2)}, u32[]{:S(2)}) collective-permute-start(f32[18,128,128]{2,1,0:T(8,128)S(1)} %get-tuple-element.298), channel_id=1, source_target_pairs={{0,16},{16,32},{32,48},{48,64},{64,80},{80,96},{96,112},{112,0},{1... | collective-permute-start | bytes 3538952 | tf_op jit(solution)/shard_map/cond/branch_2_fun/ppermute | solution.py:477
  76.2 1.6 %collective-permute-start.33 = (f32[14,128,128]{2,1,0:T(8,128)S(1)}, f32[14,128,128]{2,1,0:T(8,128)S(1)}, u32[]{:S(2)}, u32[]{:S(2)}) collective-permute-start(f32[14,128,128]{2,1,0:T(8,128)S(1)} %get-tuple-element.302), channel_id=1, source_target_pairs={{0,15},{1,0},{2,1},{3,2},{4,3},{5,4},{6,5},{7,6},{8,7},{9,8},{10,9... | collective-permute-start | bytes 2752520 | tf_op jit(solution)/shard_map/cond/branch_2_fun/ppermute | solution.py:477
  77.8 21.4 %collective-permute-done.33.z4 = f32[14,128,128]{2,1,0:T(8,128)S(1)} collective-permute-done((f32[14,128,128]{2,1,0:T(8,128)S(1)}, f32[14,128,128]{2,1,0:T(8,128)S(1)}, u32[]{:S(2)}, u32[]{:S(2)}) %collective-permute-start.33) | collective-permute-done | bytes 917536 | tf_op jit(solution)/shard_map/cond/branch_2_fun/ppermute | solution.py:477
  99.2 5.3 %collective-permute-start.35 = (f32[13,128,128]{2,1,0:T(8,128)S(1)}, f32[13,128,128]{2,1,0:T(8,128)S(1)}, u32[]{:S(2)}, u32[]{:S(2)}) collective-permute-start(f32[13,128,128]{2,1,0:T(8,128)S(1)} %get-tuple-element.306), channel_id=1, source_target_pairs={{0,15},{1,0},{2,1},{3,2},{4,3},{5,4},{6,5},{7,6},{8,7},{9,8},{10,9... | collective-permute-start | bytes 2555912 | tf_op jit(solution)/shard_map/cond/branch_2_fun/ppermute | solution.py:477
  104.5 0.0 copy-start.23
  104.5 1.4 %copy-done.23 = f32[24,128,128]{2,1,0:T(8,128)S(1)} copy-done((f32[24,128,128]{2,1,0:T(8,128)S(1)}, f32[24,128,128]{2,1,0:T(8,128)}, u32[]{:S(2)}) %copy-start.23) | copy-done | bytes 1572888 | tf_op jit(solution)/shard_map/cond
  105.9 6.1 %rest_kernel.8 = (f32[24,128,128]{2,1,0:T(8,128)}, f32[24,128,128]{2,1,0:T(8,128)S(1)}) custom-call(s32[3,1,64]{2,1,0:T(1,128)S(1)} %get-tuple-element.273.tfock, s32[3,1,64]{2,1,0:T(1,128)S(1)} %get-tuple-element.274.tfz, s32[3,1,64]{2,1,0:T(1,128)S(1)} %get-tuple-element.275.tzgt, s32[32,128]{1,0:T(8,128)S(1)} %get-tuple-element.284.plan, ...), custom_call_target="tpu_custom_call" | custom-call | flops 6442450944 | bytes 22020096 | tf_op jit(solution)/shard_map/cond/branch_2_fun/rest_kernel/pallas_call | solution.py:557
  112.1 11.4 %collective-permute-done.34.pa = f32[13,128,128]{2,1,0:T(8,128)S(1)} collective-permute-done((f32[13,128,128]{2,1,0:T(8,128)S(1)}, f32[13,128,128]{2,1,0:T(8,128)S(1)}, u32[]{:S(2)}, u32[]{:S(2)}) %collective-permute-start.34) | collective-permute-done | bytes 852000 | tf_op jit(solution)/shard_map/cond/branch_2_fun/ppermute | solution.py:477
  123.5 2.0 %join_kernel.8 = f32[24,128,128]{2,1,0:T(8,128)} custom-call(s32[32,128]{1,0:T(8,128)S(1)} %get-tuple-element.284.plan, f32[24,128,128]{2,1,0:T(8,128)S(1)} %get-tuple-element.304.part, f32[13,128,128]{2,1,0:T(8,128)S(1)} %collective-permute-done.34.pa, f32[13,128,128]{2,1,0:T(8,128)S(1)} %collective-permute-done.35.pb), custom_call_target="tpu_custom_call" | custom-call | bytes 6291456 | tf_op jit(solution)/shard_map/cond/branch_2_fun/join_kernel/pallas_call | solution.py:491
  (32 shorter events, 0.1 us)
Async XLA Ops:
  0.6 23.1 %copy-start.26 = (s32[1,1,3,64]{3,1,2,0:T(1,128)S(1)}, s32[1,1,3,64]{3,1,2,0:T(1,128)}, u32[]{:S(2)}) copy-start(s32[1,1,3,64]{3,1,2,0:T(1,128)} %param.17) | copy-start | bytes 2308
  0.6 23.1 %copy-start.27 = (s32[1,1,3,64]{3,1,2,0:T(1,128)S(1)}, s32[1,1,3,64]{3,1,2,0:T(1,128)}, u32[]{:S(2)}) copy-start(s32[1,1,3,64]{3,1,2,0:T(1,128)} %param.18) | copy-start | bytes 2308
  0.7 23.1 %copy-start.28 = (s32[1,1,3,64]{3,1,2,0:T(1,128)S(1)}, s32[1,1,3,64]{3,1,2,0:T(1,128)}, u32[]{:S(2)}) copy-start(s32[1,1,3,64]{3,1,2,0:T(1,128)} %param.19) | copy-start | bytes 2308
  0.7 23.1 %copy-start.29 = (s32[1,1,3,64]{3,1,2,0:T(1,128)S(1)}, s32[1,1,3,64]{3,1,2,0:T(1,128)}, u32[]{:S(2)}) copy-start(s32[1,1,3,64]{3,1,2,0:T(1,128)} %param.20) | copy-start | bytes 2308
  0.7 23.1 %copy-start.30 = (s32[1,1,3,64]{3,1,2,0:T(1,128)S(1)}, s32[1,1,3,64]{3,1,2,0:T(1,128)}, u32[]{:S(2)}) copy-start(s32[1,1,3,64]{3,1,2,0:T(1,128)} %param.21) | copy-start | bytes 2308
  0.7 23.1 %copy-start.31 = (f32[1,1,24,128,128]{4,3,2,1,0:T(8,128)S(1)}, f32[1,1,24,128,128]{4,3,2,1,0:T(8,128)}, u32[]{:S(2)}) copy-start(f32[1,1,24,128,128]{4,3,2,1,0:T(8,128)} %param.15) | copy-start | bytes 4718596
  24.0 2.9 %copy-start.42 = (f32[16,128,128]{2,1,0:T(8,128)S(1)}, f32[16,128,128]{2,1,0:T(8,128)}, u32[]{:S(2)}) copy-start(f32[16,128,128]{2,1,0:T(8,128)} %get-tuple-element.293) | copy-start | bytes 3145732 | tf_op jit(solution)/shard_map/cond
  26.4 36.7 %collective-permute-start.25 = (f32[24,128,128]{2,1,0:T(8,128)}, f32[24,128,128]{2,1,0:T(8,128)S(1)}, u32[]{:S(2)}, u32[]{:S(2)}) collective-permute-start(f32[24,128,128]{2,1,0:T(8,128)} %get-tuple-element.291.g0), channel_id=1, source_target_pairs={{0,112},{16,0},{32,16},{48,32},{64,48},{80,64},{96,80},{112,96},{1... | collective-permute-start | bytes 4718600 | tf_op jit(solution)/shard_map/cond/branch_2_fun/ppermute | solution.py:477
  26.4 36.7 %collective-permute-start.24 = (f32[24,128,128]{2,1,0:T(8,128)}, f32[24,128,128]{2,1,0:T(8,128)S(1)}, u32[]{:S(2)}, u32[]{:S(2)}) collective-permute-start(f32[24,128,128]{2,1,0:T(8,128)} %get-tuple-element.291.g0), channel_id=1, source_target_pairs={{0,16},{16,32},{32,48},{48,64},{64,80},{80,96},{96,112},{112,0},{1... | collective-permute-start | bytes 4718600 | tf_op jit(solution)/shard_map/cond/branch_2_fun/ppermute | solution.py:477
  26.9 28.5 %collective-permute-start.26 = (f32[16,128,128]{2,1,0:T(8,128)S(1)}, f32[16,128,128]{2,1,0:T(8,128)S(1)}, u32[]{:S(2)}, u32[]{:S(2)}) collective-permute-start(f32[16,128,128]{2,1,0:T(8,128)S(1)} %copy-done.42), channel_id=1, source_target_pairs={{0,1},{1,2},{2,3},{3,4},{4,5},{5,6},{6,7},{7,8},{8,9},{9,10},{10,1... | collective-permute-start | bytes 3145736 | tf_op jit(solution)/shard_map/cond/branch_2_fun/ppermute | solution.py:477
  27.4 35.0 %collective-permute-start.27 = (f32[16,128,128]{2,1,0:T(8,128)}, f32[16,128,128]{2,1,0:T(8,128)S(1)}, u32[]{:S(2)}, u32[]{:S(2)}) collective-permute-start(f32[16,128,128]{2,1,0:T(8,128)} %get-tuple-element.295), channel_id=1, source_target_pairs={{0,15},{1,0},{2,1},{3,2},{4,3},{5,4},{6,5},{7,6},{8,7},{9,8},{10,9... | collective-permute-start | bytes 3145736 | tf_op jit(solution)/shard_map/cond/branch_2_fun/ppermute | solution.py:477
  32.3 44.0 %collective-permute-start.32 = (f32[14,128,128]{2,1,0:T(8,128)S(1)}, f32[14,128,128]{2,1,0:T(8,128)S(1)}, u32[]{:S(2)}, u32[]{:S(2)}) collective-permute-start(f32[14,128,128]{2,1,0:T(8,128)S(1)} %get-tuple-element.301), channel_id=1, source_target_pairs={{0,1},{1,2},{2,3},{3,4},{4,5},{5,6},{6,7},{7,8},{8,9},{9,10},{10,1... | collective-permute-start | bytes 2752520 | tf_op jit(solution)/shard_map/cond/branch_2_fun/ppermute | solution.py:477
  55.5 43.7 %collective-permute-start.31 = (f32[24,128,128]{2,1,0:T(8,128)}, f32[24,128,128]{2,1,0:T(8,128)S(1)}, u32[]{:S(2)}, u32[]{:S(2)}) collective-permute-start(f32[24,128,128]{2,1,0:T(8,128)} %get-tuple-element.300.z.z0), channel_id=1, source_target_pairs={{0,112},{16,0},{32,16},{48,32},{64,48},{80,64},{96,80},{112,96},{1... | collective-permute-start | bytes 4718600 | tf_op jit(solution)/shard_map/cond/branch_2_fun/ppermute | solution.py:477
  62.4 42.1 %collective-permute-start.30 = (f32[24,128,128]{2,1,0:T(8,128)}, f32[24,128,128]{2,1,0:T(8,128)S(1)}, u32[]{:S(2)}, u32[]{:S(2)}) collective-permute-start(f32[24,128,128]{2,1,0:T(8,128)} %get-tuple-element.300.z.z0), channel_id=1, source_target_pairs={{0,16},{16,32},{32,48},{48,64},{64,80},{80,96},{96,112},{112,0},{1... | collective-permute-start | bytes 4718600 | tf_op jit(solution)/shard_map/cond/branch_2_fun/ppermute | solution.py:477
  63.1 4.0 %copy-start.2 = (f32[24,128,128]{2,1,0:T(8,128)}, f32[24,128,128]{2,1,0:T(8,128)S(1)}, u32[]{:S(2)}) copy-start(f32[24,128,128]{2,1,0:T(8,128)S(1)} %collective-permute-done.25.g2) | copy-start | bytes 4718596 | tf_op jit(solution)/shard_map/cond
  63.2 4.0 %copy-start.8 = (f32[24,128,128]{2,1,0:T(8,128)}, f32[24,128,128]{2,1,0:T(8,128)S(1)}, u32[]{:S(2)}) copy-start(f32[24,128,128]{2,1,0:T(8,128)S(1)} %collective-permute-done.24.g1) | copy-start | bytes 4718596 | tf_op jit(solution)/shard_map/cond
  71.1 1.1 copy-start.22
  72.2 32.3 %collective-permute-start.28 = (f32[18,128,128]{2,1,0:T(8,128)S(1)}, f32[18,128,128]{2,1,0:T(8,128)S(1)}, u32[]{:S(2)}, u32[]{:S(2)}) collective-permute-start(f32[18,128,128]{2,1,0:T(8,128)S(1)} %get-tuple-element.298), channel_id=1, source_target_pairs={{0,16},{16,32},{32,48},{48,64},{64,80},{80,96},{96,112},{112,0},{1... | collective-permute-start | bytes 3538952 | tf_op jit(solution)/shard_map/cond/branch_2_fun/ppermute | solution.py:477
  76.2 28.3 %collective-permute-start.29 = (f32[18,128,128]{2,1,0:T(8,128)S(1)}, f32[18,128,128]{2,1,0:T(8,128)S(1)}, u32[]{:S(2)}, u32[]{:S(2)}) collective-permute-start(f32[18,128,128]{2,1,0:T(8,128)S(1)} %get-tuple-element.299), channel_id=1, source_target_pairs={{0,112},{16,0},{32,16},{48,32},{64,48},{80,64},{96,80},{112,96},{1... | collective-permute-start | bytes 3538952 | tf_op jit(solution)/shard_map/cond/branch_2_fun/ppermute | solution.py:477
  76.2 22.9 %collective-permute-start.33 = (f32[14,128,128]{2,1,0:T(8,128)S(1)}, f32[14,128,128]{2,1,0:T(8,128)S(1)}, u32[]{:S(2)}, u32[]{:S(2)}) collective-permute-start(f32[14,128,128]{2,1,0:T(8,128)S(1)} %get-tuple-element.302), channel_id=1, source_target_pairs={{0,15},{1,0},{2,1},{3,2},{4,3},{5,4},{6,5},{7,6},{8,7},{9,8},{10,9... | collective-permute-start | bytes 2752520 | tf_op jit(solution)/shard_map/cond/branch_2_fun/ppermute | solution.py:477
  99.2 24.3 %collective-permute-start.34 = (f32[13,128,128]{2,1,0:T(8,128)S(1)}, f32[13,128,128]{2,1,0:T(8,128)S(1)}, u32[]{:S(2)}, u32[]{:S(2)}) collective-permute-start(f32[13,128,128]{2,1,0:T(8,128)S(1)} %get-tuple-element.305), channel_id=1, source_target_pairs={{0,1},{1,2},{2,3},{3,4},{4,5},{5,6},{6,7},{7,8},{8,9},{9,10},{10,1... | collective-permute-start | bytes 2555912 | tf_op jit(solution)/shard_map/cond/branch_2_fun/ppermute | solution.py:477
  99.2 5.4 %copy-start.34 = (f32[24,128,128]{2,1,0:T(8,128)}, f32[24,128,128]{2,1,0:T(8,128)S(1)}, u32[]{:S(2)}) copy-start(f32[24,128,128]{2,1,0:T(8,128)S(1)} %collective-permute-done.31.z2) | copy-start | bytes 4718596 | tf_op jit(solution)/shard_map/cond
  99.2 24.3 %collective-permute-start.35 = (f32[13,128,128]{2,1,0:T(8,128)S(1)}, f32[13,128,128]{2,1,0:T(8,128)S(1)}, u32[]{:S(2)}, u32[]{:S(2)}) collective-permute-start(f32[13,128,128]{2,1,0:T(8,128)S(1)} %get-tuple-element.306), channel_id=1, source_target_pairs={{0,15},{1,0},{2,1},{3,2},{4,3},{5,4},{6,5},{7,6},{8,7},{9,8},{10,9... | collective-permute-start | bytes 2555912 | tf_op jit(solution)/shard_map/cond/branch_2_fun/ppermute | solution.py:477
  104.5 1.4 %copy-start.23 = (f32[24,128,128]{2,1,0:T(8,128)S(1)}, f32[24,128,128]{2,1,0:T(8,128)}, u32[]{:S(2)}) copy-start(f32[24,128,128]{2,1,0:T(8,128)} %copy-done.22) | copy-start | bytes 4718596 | tf_op jit(solution)/shard_map/cond

commit v3 on v2

--- a/solution.py
+++ b/solution.py
@@ -522,8 +522,9 @@
     z3, z4 = pack(pick, z)
     g_late, z_late, z3, z4 = lax.optimization_barrier((g, z, z3, z4))
     gn = (shifted(g_late, "gx", 1), shifted(g_late, "gx", -1), ga[0], gy[0], ga[1], gy[1])
-    zn = (shifted(z_late, "gx", 1), shifted(z_late, "gx", -1), shifted(z3, "gy", 1), shifted(z4, "gy", -1))
-    plan, fs, ft, zs = pl.pallas_call(
+    zy = (shifted(z3, "gy", 1), shifted(z4, "gy", -1))
+    zn = (shifted(z_late, "gx", 1), shifted(z_late, "gx", -1)) + zy
+    make_plan = pl.pallas_call(
         functools.partial(plan_kernel, lead=ga[0].shape[0]),
         name="plan_kernel",
         out_shape=[jax.ShapeDtypeStruct((PLAN_ROWS, TILE), I32)] + [cut_tiles(per_cell)] * 3,
@@ -532,7 +533,8 @@
         scratch_shapes=[pltpu.VMEM((8, cap), F32), pltpu.VMEM((3, per_cell, TILE, 2 * TILE), jnp.bfloat16), DMA((3,))],
         compiler_params=pltpu.CompilerParams(vmem_limit_bytes=24 * 2**20),
         cost_estimate=cost(cap, 8 * per_cell),
-    )(tzg, tfock, tfz, tzgt, ttrans, *tn, f, z)
+    )
+    plan, fs, ft, zs = make_plan(tzg, tfock, tfz, tzgt, ttrans, *tn, f, z)
     ws = pl.pallas_call(
         w_kernel,
         name="w_kernel",

time: 126 us -> 126 us (level)
  no operation moved by 1% of the time
where the time goes in v3:
time: 126 us
  waiting for transfers between devices  56 us (44%)
  Pallas kernels  46.7 us (37%)
  starting transfers between devices  18.5 us (15%)
  local copies, waits for them, and re-layouts  2.58 us (2%)
  between operations  1.58 us (1%)
    ppermute x12, waiting for transfers between devices, shifted(): return lax.ppermute(array, axis, [(i, (i + by) % n) for i in range(n)])  56 us
    pallas_call x1, Pallas kernels, body(): pl.pallas_call(functools.partial(meet_kernel, rooms=rooms, lead=lead, cut...  22.4 us
    ppermute x12, starting transfers between devices, shifted(): return lax.ppermute(array, axis, [(i, (i + by) % n) for i in range(n)])  18.5 us
    pallas_call x1, Pallas kernels, finish(): pl.pallas_call(rest_kernel, name='rest_kernel', out_shape=[pltpu.HBM((per...  6.11 us
    pallas_call x1, Pallas kernels, finish(): plan, fs, ft, zs = make_plan(tzg, tfock, tfz, tzgt, ttrans, *tn, f, z)  5.92 us
    pallas_call x1, Pallas kernels, finish(): pl.pallas_call(w_kernel, name='w_kernel', out_shape=cut_tiles(per_cell),...  4 us
    pallas_call x1, Pallas kernels, finish(): pl.pallas_call(p_kernel, name='p_kernel', out_shape=[tiles(n) for n in (p...  3.9 us
    cond x12, local copies, waits for them, and re-layouts  2.56 us
  transfers between devices with their start and end apart: 12, of which 3 were waited for; matrix products, arithmetic and copies ran while one was open for 0% of the time, Pallas kernels for 16%

profile of v3, /device:TPU:24, one launch (start us, length us, event | category | flops | bytes accessed | tf_op | source)
XLA Modules:
  0.0 126.2 jit_solution(16450569541018852074)
XLA Ops:
  0.7 22.4 %meet_kernel.1 = (f32[8,128,128]{2,1,0:T(8,128)S(1)}, f32[8,128,128]{2,1,0:T(8,128)S(1)}, s32[3,1,64]{2,1,0:T(1,128)S(1)}, s32[3,1,64]{2,1,0:T(1,128)S(1)}, s32[...) custom-call(s32[3,1,64]{2,1,0:T(1,128)} %bitcast.22, ...), custom_call_target="tpu_custom_call" | custom-call | tf_op jit(solution)/shard_map/meet_kernel/pallas_call | solution.py:595
  23.8 102.2 %conditional.1 = (f32[24,128,128]{2,1,0:T(8,128)}, f32[1,1,24,128,128]{4,3,2,1,0:T(8,128)}) conditional(s32[]{:T(128)} %bitcast.13, (s32[3,1,64]{2,1,0:T(1,128)S(1)}, s32[3,1,64]{2,1,0:T(1,128)S(1)}, s32[3,1,64]{2,1,0:T(1,128)S(1)}, s32[3,1,64]{2,1,0:T(1,128)S(1)}, s32[3,1,64]{2,1,0:T(1,128)S(1)}, ...), branch_computations={%region_0.0_spmd, %region_1.0_spmd, %region_2.0_spmd, %region_3.0_... | conditional | flops 15032385536 | bytes 195035856 | solution.py:627
  24.0 2.4 %pack_kernel.8 = (f32[14,128,128]{2,1,0:T(8,128)S(1)}, f32[14,128,128]{2,1,0:T(8,128)S(1)}) custom-call(s32[8,128]{1,0:T(8,128)S(1)} %get-tuple-element.288.pick, f32[24,128,128]{2,1,0:T(8,128)} %get-tuple-element.300.z.z0), custom_call_target="tpu_custom_call" | custom-call | bytes 6291456 | tf_op jit(solution)/shard_map/cond/branch_2_fun/pack_kernel/pallas_call | solution.py:522
  26.4 0.0 collective-permute-start.25
  26.4 0.5 collective-permute-start.24
  26.9 0.5 collective-permute-start.26
  27.4 4.9 %collective-permute-start.27 = (f32[16,128,128]{2,1,0:T(8,128)}, f32[16,128,128]{2,1,0:T(8,128)S(1)}, u32[]{:S(2)}, u32[]{:S(2)}) collective-permute-start(f32[16,128,128]{2,1,0:T(8,128)} %get-tuple-element.295), channel_id=1, source_target_pairs={{0,15},{1,0},{2,1},{3,2},{4,3},{5,4},{6,5},{7,6},{8,7},{9,8},{10,9... | collective-permute-start | bytes 3145736 | tf_op jit(solution)/shard_map/cond/branch_2_fun/ppermute | solution.py:477
  32.3 23.2 %collective-permute-done.26.g3 = f32[16,128,128]{2,1,0:T(8,128)S(1)} collective-permute-done((f32[16,128,128]{2,1,0:T(8,128)S(1)}, f32[16,128,128]{2,1,0:T(8,128)S(1)}, u32[]{:S(2)}, u32[]{:S(2)}) %collective-permute-start.26) | collective-permute-done | bytes 1048608 | tf_op jit(solution)/shard_map/cond/branch_2_fun/ppermute | solution.py:477
  55.5 1.1 collective-permute-start.31
  56.5 5.9 %plan_kernel.8 = (s32[32,128]{1,0:T(8,128)S(1)}, bf16[24,128,256]{2,1,0:T(8,128)(2,1)S(1)}, bf16[24,128,256]{2,1,0:T(8,128)(2,1)S(1)}, bf16[24,128,256]{2,1,0:T(8,128)(2,1)S(1)}) custom-call(s32[3,1,64]{2,1,0:T(1,128)S(1)} %get-tuple-element.276.tzg.tasks, s32[3,1,64]{2,1,0:T(1,128)S(1)} %get-tuple-element.273.tfock, ...), custom_call_target="tpu_custom_call" | custom-call | flops 2147483648 | bytes 12582912 | tf_op jit(solution)/shard_map/cond/branch_2_fun/plan_kernel/pallas_call | solution.py:537
  62.4 0.7 collective-permute-start.30
  63.2 4.0 %w_kernel.8.ws = bf16[24,128,256]{2,1,0:T(8,128)(2,1)S(1)} custom-call(s32[3,1,64]{2,1,0:T(1,128)S(1)} %get-tuple-element.276.tzg.tasks, s32[32,128]{1,0:T(8,128)S(1)} %get-tuple-element.284.plan, bf16[24,128,256]{2,1,0:T(8,128)(2,1)S(1)} %get-tuple-element.286.zs, f32[24,128,128]{2,1,0:T(8,128)} %get-tuple-element.291.g0, ...), custom_call_target="tpu_custom_call" | custom-call | flops 2147483648 | bytes 11010048 | tf_op jit(solution)/shard_map/cond/branch_2_fun/w_kernel/pallas_call | solution.py:538
  67.2 3.9 %p_kernel.8 = (f32[24,128,128]{2,1,0:T(8,128)S(1)}, f32[18,128,128]{2,1,0:T(8,128)S(1)}, f32[18,128,128]{2,1,0:T(8,128)S(1)}, f32[13,128,128]{2,1,0:T(8,128)S(1)}, f32[13,128,128]{2,1,0:T(8,128)S(1)}) custom-call(s32[32,128]{1,0:T(8,128)S(1)} %get-tuple-element.284.plan, bf16[24,128,256]{2,1,0:T(8,128)(2,1)S(1)} %get-tuple-element.296.ft, ...), custom_call_target="tpu_custom_call" | custom-call | flops 4294967296 | bytes 11010048 | tf_op jit(solution)/shard_map/cond/branch_2_fun/p_kernel/pallas_call | solution.py:548
  71.1 0.0 copy-start.22
  71.1 1.1 copy-done.22
  72.2 4.0 %collective-permute-start.28 = (f32[18,128,128]{2,1,0:T(8,128)S(1)}, f32[18,128,128]{2,1,0:T(8,128)S(1)}, u32[]{:S(2)}, u32[]{:S(2)}) collective-permute-start(f32[18,128,128]{2,1,0:T(8,128)S(1)} %get-tuple-element.298), channel_id=1, source_target_pairs={{0,16},{16,32},{32,48},{48,64},{64,80},{80,96},{96,112},{112,0},{1... | collective-permute-start | bytes 3538952 | tf_op jit(solution)/shard_map/cond/branch_2_fun/ppermute | solution.py:477
  76.2 1.6 %collective-permute-start.33 = (f32[14,128,128]{2,1,0:T(8,128)S(1)}, f32[14,128,128]{2,1,0:T(8,128)S(1)}, u32[]{:S(2)}, u32[]{:S(2)}) collective-permute-start(f32[14,128,128]{2,1,0:T(8,128)S(1)} %get-tuple-element.302), channel_id=1, source_target_pairs={{0,15},{1,0},{2,1},{3,2},{4,3},{5,4},{6,5},{7,6},{8,7},{9,8},{10,9... | collective-permute-start | bytes 2752520 | tf_op jit(solution)/shard_map/cond/branch_2_fun/ppermute | solution.py:477
  77.8 21.4 %collective-permute-done.33.z4 = f32[14,128,128]{2,1,0:T(8,128)S(1)} collective-permute-done((f32[14,128,128]{2,1,0:T(8,128)S(1)}, f32[14,128,128]{2,1,0:T(8,128)S(1)}, u32[]{:S(2)}, u32[]{:S(2)}) %collective-permute-start.33) | collective-permute-done | bytes 917536 | tf_op jit(solution)/shard_map/cond/branch_2_fun/ppermute | solution.py:477
  99.2 5.3 %collective-permute-start.35 = (f32[13,128,128]{2,1,0:T(8,128)S(1)}, f32[13,128,128]{2,1,0:T(8,128)S(1)}, u32[]{:S(2)}, u32[]{:S(2)}) collective-permute-start(f32[13,128,128]{2,1,0:T(8,128)S(1)} %get-tuple-element.306), channel_id=1, source_target_pairs={{0,15},{1,0},{2,1},{3,2},{4,3},{5,4},{6,5},{7,6},{8,7},{9,8},{10,9... | collective-permute-start | bytes 2555912 | tf_op jit(solution)/shard_map/cond/branch_2_fun/ppermute | solution.py:477
  104.5 0.0 copy-start.23
  104.5 1.4 %copy-done.23 = f32[24,128,128]{2,1,0:T(8,128)S(1)} copy-done((f32[24,128,128]{2,1,0:T(8,128)S(1)}, f32[24,128,128]{2,1,0:T(8,128)}, u32[]{:S(2)}) %copy-start.23) | copy-done | bytes 1572888 | tf_op jit(solution)/shard_map/cond
  105.9 6.1 %rest_kernel.8 = (f32[24,128,128]{2,1,0:T(8,128)}, f32[24,128,128]{2,1,0:T(8,128)S(1)}) custom-call(s32[3,1,64]{2,1,0:T(1,128)S(1)} %get-tuple-element.273.tfock, s32[3,1,64]{2,1,0:T(1,128)S(1)} %get-tuple-element.274.tfz, s32[3,1,64]{2,1,0:T(1,128)S(1)} %get-tuple-element.275.tzgt, s32[32,128]{1,0:T(8,128)S(1)} %get-tuple-element.284.plan, ...), custom_call_target="tpu_custom_call" | custom-call | flops 6442450944 | bytes 22020096 | tf_op jit(solution)/shard_map/cond/branch_2_fun/rest_kernel/pallas_call | solution.py:559
  112.1 11.4 %collective-permute-done.34.pa = f32[13,128,128]{2,1,0:T(8,128)S(1)} collective-permute-done((f32[13,128,128]{2,1,0:T(8,128)S(1)}, f32[13,128,128]{2,1,0:T(8,128)S(1)}, u32[]{:S(2)}, u32[]{:S(2)}) %collective-permute-start.34) | collective-permute-done | bytes 852000 | tf_op jit(solution)/shard_map/cond/branch_2_fun/ppermute | solution.py:477
  123.5 2.0 %join_kernel.8 = f32[24,128,128]{2,1,0:T(8,128)} custom-call(s32[32,128]{1,0:T(8,128)S(1)} %get-tuple-element.284.plan, f32[24,128,128]{2,1,0:T(8,128)S(1)} %get-tuple-element.304.part, f32[13,128,128]{2,1,0:T(8,128)S(1)} %collective-permute-done.34.pa, f32[13,128,128]{2,1,0:T(8,128)S(1)} %collective-permute-done.35.pb), custom_call_target="tpu_custom_call" | custom-call | bytes 6291456 | tf_op jit(solution)/shard_map/cond/branch_2_fun/join_kernel/pallas_call | solution.py:491
  (32 shorter events, 0.1 us)
Async XLA Ops:
  0.6 23.1 %copy-start.26 = (s32[1,1,3,64]{3,1,2,0:T(1,128)S(1)}, s32[1,1,3,64]{3,1,2,0:T(1,128)}, u32[]{:S(2)}) copy-start(s32[1,1,3,64]{3,1,2,0:T(1,128)} %param.17) | copy-start | bytes 2308
  0.6 23.1 %copy-start.27 = (s32[1,1,3,64]{3,1,2,0:T(1,128)S(1)}, s32[1,1,3,64]{3,1,2,0:T(1,128)}, u32[]{:S(2)}) copy-start(s32[1,1,3,64]{3,1,2,0:T(1,128)} %param.18) | copy-start | bytes 2308
  0.7 23.1 %copy-start.28 = (s32[1,1,3,64]{3,1,2,0:T(1,128)S(1)}, s32[1,1,3,64]{3,1,2,0:T(1,128)}, u32[]{:S(2)}) copy-start(s32[1,1,3,64]{3,1,2,0:T(1,128)} %param.19) | copy-start | bytes 2308
  0.7 23.1 %copy-start.29 = (s32[1,1,3,64]{3,1,2,0:T(1,128)S(1)}, s32[1,1,3,64]{3,1,2,0:T(1,128)}, u32[]{:S(2)}) copy-start(s32[1,1,3,64]{3,1,2,0:T(1,128)} %param.20) | copy-start | bytes 2308
  0.7 23.1 %copy-start.30 = (s32[1,1,3,64]{3,1,2,0:T(1,128)S(1)}, s32[1,1,3,64]{3,1,2,0:T(1,128)}, u32[]{:S(2)}) copy-start(s32[1,1,3,64]{3,1,2,0:T(1,128)} %param.21) | copy-start | bytes 2308
  0.7 23.1 %copy-start.31 = (f32[1,1,24,128,128]{4,3,2,1,0:T(8,128)S(1)}, f32[1,1,24,128,128]{4,3,2,1,0:T(8,128)}, u32[]{:S(2)}) copy-start(f32[1,1,24,128,128]{4,3,2,1,0:T(8,128)} %param.15) | copy-start | bytes 4718596
  24.0 2.9 %copy-start.42 = (f32[16,128,128]{2,1,0:T(8,128)S(1)}, f32[16,128,128]{2,1,0:T(8,128)}, u32[]{:S(2)}) copy-start(f32[16,128,128]{2,1,0:T(8,128)} %get-tuple-element.293) | copy-start | bytes 3145732 | tf_op jit(solution)/shard_map/cond
  26.4 36.7 %collective-permute-start.25 = (f32[24,128,128]{2,1,0:T(8,128)}, f32[24,128,128]{2,1,0:T(8,128)S(1)}, u32[]{:S(2)}, u32[]{:S(2)}) collective-permute-start(f32[24,128,128]{2,1,0:T(8,128)} %get-tuple-element.291.g0), channel_id=1, source_target_pairs={{0,112},{16,0},{32,16},{48,32},{64,48},{80,64},{96,80},{112,96},{1... | collective-permute-start | bytes 4718600 | tf_op jit(solution)/shard_map/cond/branch_2_fun/ppermute | solution.py:477
  26.4 36.7 %collective-permute-start.24 = (f32[24,128,128]{2,1,0:T(8,128)}, f32[24,128,128]{2,1,0:T(8,128)S(1)}, u32[]{:S(2)}, u32[]{:S(2)}) collective-permute-start(f32[24,128,128]{2,1,0:T(8,128)} %get-tuple-element.291.g0), channel_id=1, source_target_pairs={{0,16},{16,32},{32,48},{48,64},{64,80},{80,96},{96,112},{112,0},{1... | collective-permute-start | bytes 4718600 | tf_op jit(solution)/shard_map/cond/branch_2_fun/ppermute | solution.py:477
  26.9 28.5 %collective-permute-start.26 = (f32[16,128,128]{2,1,0:T(8,128)S(1)}, f32[16,128,128]{2,1,0:T(8,128)S(1)}, u32[]{:S(2)}, u32[]{:S(2)}) collective-permute-start(f32[16,128,128]{2,1,0:T(8,128)S(1)} %copy-done.42), channel_id=1, source_target_pairs={{0,1},{1,2},{2,3},{3,4},{4,5},{5,6},{6,7},{7,8},{8,9},{9,10},{10,1... | collective-permute-start | bytes 3145736 | tf_op jit(solution)/shard_map/cond/branch_2_fun/ppermute | solution.py:477
  27.4 35.0 %collective-permute-start.27 = (f32[16,128,128]{2,1,0:T(8,128)}, f32[16,128,128]{2,1,0:T(8,128)S(1)}, u32[]{:S(2)}, u32[]{:S(2)}) collective-permute-start(f32[16,128,128]{2,1,0:T(8,128)} %get-tuple-element.295), channel_id=1, source_target_pairs={{0,15},{1,0},{2,1},{3,2},{4,3},{5,4},{6,5},{7,6},{8,7},{9,8},{10,9... | collective-permute-start | bytes 3145736 | tf_op jit(solution)/shard_map/cond/branch_2_fun/ppermute | solution.py:477
  32.3 44.0 %collective-permute-start.32 = (f32[14,128,128]{2,1,0:T(8,128)S(1)}, f32[14,128,128]{2,1,0:T(8,128)S(1)}, u32[]{:S(2)}, u32[]{:S(2)}) collective-permute-start(f32[14,128,128]{2,1,0:T(8,128)S(1)} %get-tuple-element.301), channel_id=1, source_target_pairs={{0,1},{1,2},{2,3},{3,4},{4,5},{5,6},{6,7},{7,8},{8,9},{9,10},{10,1... | collective-permute-start | bytes 2752520 | tf_op jit(solution)/shard_map/cond/branch_2_fun/ppermute | solution.py:477
  55.5 43.7 %collective-permute-start.31 = (f32[24,128,128]{2,1,0:T(8,128)}, f32[24,128,128]{2,1,0:T(8,128)S(1)}, u32[]{:S(2)}, u32[]{:S(2)}) collective-permute-start(f32[24,128,128]{2,1,0:T(8,128)} %get-tuple-element.300.z.z0), channel_id=1, source_target_pairs={{0,112},{16,0},{32,16},{48,32},{64,48},{80,64},{96,80},{112,96},{1... | collective-permute-start | bytes 4718600 | tf_op jit(solution)/shard_map/cond/branch_2_fun/ppermute | solution.py:477
  62.4 42.1 %collective-permute-start.30 = (f32[24,128,128]{2,1,0:T(8,128)}, f32[24,128,128]{2,1,0:T(8,128)S(1)}, u32[]{:S(2)}, u32[]{:S(2)}) collective-permute-start(f32[24,128,128]{2,1,0:T(8,128)} %get-tuple-element.300.z.z0), channel_id=1, source_target_pairs={{0,16},{16,32},{32,48},{48,64},{64,80},{80,96},{96,112},{112,0},{1... | collective-permute-start | bytes 4718600 | tf_op jit(solution)/shard_map/cond/branch_2_fun/ppermute | solution.py:477
  63.1 4.0 %copy-start.2 = (f32[24,128,128]{2,1,0:T(8,128)}, f32[24,128,128]{2,1,0:T(8,128)S(1)}, u32[]{:S(2)}) copy-start(f32[24,128,128]{2,1,0:T(8,128)S(1)} %collective-permute-done.25.g2) | copy-start | bytes 4718596 | tf_op jit(solution)/shard_map/cond
  63.2 4.0 %copy-start.8 = (f32[24,128,128]{2,1,0:T(8,128)}, f32[24,128,128]{2,1,0:T(8,128)S(1)}, u32[]{:S(2)}) copy-start(f32[24,128,128]{2,1,0:T(8,128)S(1)} %collective-permute-done.24.g1) | copy-start | bytes 4718596 | tf_op jit(solution)/shard_map/cond
  71.1 1.1 copy-start.22
  72.2 32.3 %collective-permute-start.28 = (f32[18,128,128]{2,1,0:T(8,128)S(1)}, f32[18,128,128]{2,1,0:T(8,128)S(1)}, u32[]{:S(2)}, u32[]{:S(2)}) collective-permute-start(f32[18,128,128]{2,1,0:T(8,128)S(1)} %get-tuple-element.298), channel_id=1, source_target_pairs={{0,16},{16,32},{32,48},{48,64},{64,80},{80,96},{96,112},{112,0},{1... | collective-permute-start | bytes 3538952 | tf_op jit(solution)/shard_map/cond/branch_2_fun/ppermute | solution.py:477
  76.2 28.3 %collective-permute-start.29 = (f32[18,128,128]{2,1,0:T(8,128)S(1)}, f32[18,128,128]{2,1,0:T(8,128)S(1)}, u32[]{:S(2)}, u32[]{:S(2)}) collective-permute-start(f32[18,128,128]{2,1,0:T(8,128)S(1)} %get-tuple-element.299), channel_id=1, source_target_pairs={{0,112},{16,0},{32,16},{48,32},{64,48},{80,64},{96,80},{112,96},{1... | collective-permute-start | bytes 3538952 | tf_op jit(solution)/shard_map/cond/branch_2_fun/ppermute | solution.py:477
  76.2 22.9 %collective-permute-start.33 = (f32[14,128,128]{2,1,0:T(8,128)S(1)}, f32[14,128,128]{2,1,0:T(8,128)S(1)}, u32[]{:S(2)}, u32[]{:S(2)}) collective-permute-start(f32[14,128,128]{2,1,0:T(8,128)S(1)} %get-tuple-element.302), channel_id=1, source_target_pairs={{0,15},{1,0},{2,1},{3,2},{4,3},{5,4},{6,5},{7,6},{8,7},{9,8},{10,9... | collective-permute-start | bytes 2752520 | tf_op jit(solution)/shard_map/cond/branch_2_fun/ppermute | solution.py:477
  99.2 24.3 %collective-permute-start.34 = (f32[13,128,128]{2,1,0:T(8,128)S(1)}, f32[13,128,128]{2,1,0:T(8,128)S(1)}, u32[]{:S(2)}, u32[]{:S(2)}) collective-permute-start(f32[13,128,128]{2,1,0:T(8,128)S(1)} %get-tuple-element.305), channel_id=1, source_target_pairs={{0,1},{1,2},{2,3},{3,4},{4,5},{5,6},{6,7},{7,8},{8,9},{9,10},{10,1... | collective-permute-start | bytes 2555912 | tf_op jit(solution)/shard_map/cond/branch_2_fun/ppermute | solution.py:477
  99.2 5.4 %copy-start.34 = (f32[24,128,128]{2,1,0:T(8,128)}, f32[24,128,128]{2,1,0:T(8,128)S(1)}, u32[]{:S(2)}) copy-start(f32[24,128,128]{2,1,0:T(8,128)S(1)} %collective-permute-done.31.z2) | copy-start | bytes 4718596 | tf_op jit(solution)/shard_map/cond
  99.2 24.3 %collective-permute-start.35 = (f32[13,128,128]{2,1,0:T(8,128)S(1)}, f32[13,128,128]{2,1,0:T(8,128)S(1)}, u32[]{:S(2)}, u32[]{:S(2)}) collective-permute-start(f32[13,128,128]{2,1,0:T(8,128)S(1)} %get-tuple-element.306), channel_id=1, source_target_pairs={{0,15},{1,0},{2,1},{3,2},{4,3},{5,4},{6,5},{7,6},{8,7},{9,8},{10,9... | collective-permute-start | bytes 2555912 | tf_op jit(solution)/shard_map/cond/branch_2_fun/ppermute | solution.py:477
  104.5 1.4 %copy-start.23 = (f32[24,128,128]{2,1,0:T(8,128)S(1)}, f32[24,128,128]{2,1,0:T(8,128)}, u32[]{:S(2)}) copy-start(f32[24,128,128]{2,1,0:T(8,128)} %copy-done.22) | copy-start | bytes 4718596 | tf_op jit(solution)/shard_map/cond
